TPU v7x, 512 devices: a whole 4x4x16 slice. The times are simulated.
512 devices in a mesh: expert: 64 (over x, z), tensor: 8 (over y, core).
Axes of the slice: x: 4, y: 4, z: 16, core: 2. Of those that a mesh axis runs over, the one named last changes fastest.
Arguments:
- tokens: bfloat16 [1024, 7168], P('expert', 'tensor'), may hold values from -6 to 6
- expert_ids: int32 [1024, 8], P('expert'), may hold values from 0 to 31, as said below
- route_weights: float32 [1024, 8], P('expert'), may hold values from 0.05 to 1
- gate_weight: bfloat16 [64, 512, 7168], P('expert', 'tensor'), may hold values from -0.0625 to 0.0625
- up_weight: bfloat16 [64, 512, 7168], P('expert', 'tensor'), may hold values from -0.0625 to 0.0625
- down_weight: bfloat16 [64, 512, 7168], P('expert', 'tensor'), may hold values from -0.1875 to 0.1875
Outputs:
- mixed: bfloat16 [1024, 7168], P('expert', 'tensor')
Inputs may be any that keep to these rules, and one draw needn't show every extreme that they name: `expert_ids`: each row holds 8 different experts. One expert, the same for all tokens, is named by exactly 4 of the 16 tokens of every block of 16 consecutive tokens; every other expert by at most 4 tokens of a block.
All inputs are finite; a program needn't handle non-finite values.
Results may differ from a plain program's by a relative error of at most 0.015.
Values may be sent and summed in bfloat16 or wider, within the bound.
No kernel may reach another device: no remote copies, remote signals or barrier semaphores. Data moves between devices by JAX's collectives and lax.ppermute only.
A program may use at most 64 MiB of HBM per device.

v0:
```python
import jax
import jax.numpy as jnp
from jax import lax
from jax.experimental import pallas as pl
from jax.experimental.pallas import tpu as pltpu
from jax.sharding import PartitionSpec as P

F32 = jnp.float32
BF16 = jnp.bfloat16


def slot_onehot(ids, slots, capacity, copies):
    per_token, tok_count = ids.shape
    slot = lax.broadcasted_iota(jnp.int32, (slots, tok_count), 0)
    expert = slot // (capacity * copies)
    hit = jnp.zeros((slots, tok_count), F32)
    for j in range(per_token):
        hit = hit + jnp.where(ids[j : j + 1, :] == expert, 1.0, 0.0)
    row = lax.broadcasted_iota(jnp.int32, (tok_count, tok_count), 0)
    col = lax.broadcasted_iota(jnp.int32, (tok_count, tok_count), 1)
    before = jnp.where(row < col, 1.0, 0.0).astype(BF16)
    earlier = jnp.dot(hit.astype(BF16), before, preferred_element_type=F32)
    rank = (slot % capacity).astype(F32)
    return jnp.where((hit > 0.5) & (earlier == rank), 1.0, 0.0), expert


def pack_kernel(copies, ring, ids_ref, tok_ref, gate_ref, up_ref, out_ref, block_ref, *refs):
    ids, tok, packed, held, taken, given, small = refs
    fetches = [
        pltpu.make_async_copy(ids_ref, ids, small.at[0]),
        pltpu.make_async_copy(tok_ref, tok, small.at[1]),
    ]
    for fetch in fetches:
        fetch.start()
    reads = cut_reads(ring, (gate_ref, up_ref), held, taken)
    peers, capacity, width = packed.shape
    for fetch in fetches:
        fetch.wait()
    select, _ = slot_onehot(ids[...], peers * capacity, capacity, copies)
    rows = jnp.dot(select.astype(BF16), tok[...], preferred_element_type=F32)
    packed[...] = rows.reshape(peers, capacity, width).astype(BF16)
    for read in reads:
        read.wait()
    writes = [
        pltpu.make_async_copy(held, block_ref, given.at[0]),
        pltpu.make_async_copy(packed, out_ref, given.at[1]),
    ]
    for write in writes:
        write.start()
    for write in writes:
        write.wait()


def mix_kernel(capacity, copies, ids_ref, route_ref, mix_ref):
    ids = ids_ref[...]
    route = route_ref[...]
    select, expert = slot_onehot(ids, mix_ref.shape[0], capacity, copies)
    weight = jnp.zeros(select.shape, F32)
    for j in range(ids.shape[0]):
        weight = weight + jnp.where(ids[j : j + 1, :] == expert, route[j : j + 1, :], 0.0)
    mix_ref[...] = select * weight


def combine_kernel(mix_ref, rows_ref, out_ref):
    mix = mix_ref[...]
    high = mix.astype(BF16)
    low = (mix - high.astype(F32)).astype(BF16)
    rows = rows_ref[...]
    dims = (((0,), (0,)), ((), ()))
    total = lax.dot_general(high, rows, dims, preferred_element_type=F32)
    total = total + lax.dot_general(low, rows, dims, preferred_element_type=F32)
    out_ref[...] = total.astype(BF16)


CORES = 2
VMEM_BYTES = 10 * 2**20


def moved_by(index, groups, ring, core, sign=1):
    rings = groups // CORES
    place = lax.rem(index // CORES + sign * ring + rings, rings)
    return place * CORES + lax.rem(lax.rem(index, CORES) + core, CORES)


def shift_pairs(groups, ring, core):
    rings = groups // CORES
    return [
        (i, (i // CORES + ring) % rings * CORES + (i + core) % CORES) for i in range(groups)
    ]


def cut_reads(ring, weights, held, taken):
    wide = held.shape[1]
    units, full = weights[0].shape
    rings = full // wide
    chip = lax.axis_index("tensor") // CORES
    cols = pl.ds(pl.multiple_of(lax.rem(chip + ring, rings) * wide, 128), wide)
    reads = []
    for part, weight in enumerate(weights):
        reads.append(
            pltpu.make_async_copy(
                weight.at[:, cols], held.at[pl.ds(part * units, units), :], taken.at[part]
            )
        )
        reads[-1].start()
    return reads


def cut_kernel(pieces, gate_ref, up_ref, down_ref, *refs):
    outs, refs = refs[: len(pieces)], refs[len(pieces) :]
    held, (taken, given) = refs[:-2], refs[-2:]
    reads = []
    for place, (which, ring) in enumerate(pieces):
        weights = (gate_ref, up_ref) if which == "up" else (down_ref,)
        reads.append(cut_reads(ring, weights, held[place], taken.at[place]))
    writes = []
    for place, out in enumerate(outs):
        for read in reads[place]:
            read.wait()
        writes.append(pltpu.make_async_copy(held[place], out, given.at[place]))
        writes[-1].start()
    for write in writes:
        write.wait()


def cut(pieces, gate, up, down, wide):
    units = gate.shape[0]
    shapes = [(2 * units if which == "up" else units, wide) for which, _ in pieces]
    whole = pl.BlockSpec(memory_space=pl.ANY)
    return pl.pallas_call(
        lambda *refs: cut_kernel(pieces, *refs),
        out_shape=[jax.ShapeDtypeStruct(shape, BF16) for shape in shapes],
        in_specs=[whole] * 3,
        out_specs=[whole] * len(pieces),
        scratch_shapes=[pltpu.VMEM(shape, BF16) for shape in shapes]
        + [
            pltpu.SemaphoreType.DMA((len(pieces), 2)),
            pltpu.SemaphoreType.DMA((len(pieces),)),
        ],
        name="cut",
    )(gate, up, down)


def half_product(block_ref, rows_ref, half):
    width = rows_ref.shape[1]
    cols = pl.ds(pl.multiple_of(half * width, 128), width)
    return lax.dot_general(
        block_ref[:, cols], rows_ref[...], (((1,), (1,)), ((), ())), preferred_element_type=F32
    )


def near_kernel(rows_ref, *refs):
    *blocks, out_ref = refs
    chip, core = lax.axis_index("tensor") // CORES, lax.rem(lax.axis_index("tensor"), CORES)
    for ring, block in enumerate(blocks):
        source = lax.rem(chip - ring + len(blocks), len(blocks))
        out_ref[source] = half_product(block, rows_ref, core)


def far_kernel(rows_ref, near_ref, *refs):
    *blocks, out_ref = refs
    chip, core = lax.axis_index("tensor") // CORES, lax.rem(lax.axis_index("tensor"), CORES)
    for ring, block in enumerate(blocks):
        source = lax.rem(chip - ring + len(blocks), len(blocks))
        out_ref[source] = (near_ref[source] + half_product(block, rows_ref, 1 - core)).astype(BF16)


def hidden_kernel(partial_ref, out_ref):
    groups, units, _ = out_ref.shape
    act = partial_ref[0].astype(F32)
    for g in range(1, partial_ref.shape[0]):
        act = act + partial_ref[g].astype(F32)
    gate, up = act[:units], act[units:]
    hidden = (jax.nn.silu(gate) * up).astype(BF16)
    for g in range(groups):
        out_ref[g] = hidden


def core_cut_kernel(*refs):
    *blocks, near_ref, far_ref = refs
    core = lax.rem(lax.axis_index("tensor"), CORES)
    units = blocks[0].shape[0]
    width = near_ref.shape[1]
    for ring, block in enumerate(blocks):
        rows = pl.ds(ring * units, units)
        near_ref[rows, :] = block[:, pl.ds(pl.multiple_of(core * width, 128), width)]
        far_ref[rows, :] = block[:, pl.ds(pl.multiple_of((1 - core) * width, 128), width)]


def down_columns(blocks, width, groups):
    units, rings = blocks[0].shape[0], len(blocks)
    for ring in range(1, rings):
        blocks[ring] = lax.ppermute(
            blocks[ring], "tensor", shift_pairs(groups, ring, 0)
        )
    near, far = pl.pallas_call(
        core_cut_kernel,
        out_shape=[jax.ShapeDtypeStruct((rings * units, width), BF16)] * 2,
        compiler_params=pltpu.CompilerParams(vmem_limit_bytes=VMEM_BYTES),
        name="core_cut",
    )(*[blocks[ring] for ring in range(rings)])
    return near, lax.ppermute(far, "tensor", shift_pairs(groups, 0, 1))


def down_kernel(hidden_ref, near_ref, far_ref, keep_ref, give_ref, held, rows):
    groups, units, _ = hidden_ref.shape
    me = lax.axis_index("tensor")
    for core in range(CORES):
        for ring in range(groups // CORES):
            source = moved_by(me, groups, ring, core, sign=-1)
            held[core, pl.ds(ring * units, units), :] = hidden_ref[source]
    dims = (((0,), (0,)), ((), ()))
    total = lax.dot_general(held[0], near_ref[...], dims, preferred_element_type=F32)
    total = total + lax.dot_general(held[1], far_ref[...], dims, preferred_element_type=F32)
    rows[...] = total.reshape(rows.shape)
    slots = keep_ref.shape[1]
    half = lax.rem(lax.axis_index("expert"), 2)
    low, high = rows[:, :slots, :], rows[:, slots:, :]
    keep_ref[...] = jnp.where(half == 0, low, high).astype(BF16)
    give_ref[...] = jnp.where(half == 0, high, low).astype(BF16)


def body(tokens, expert_ids, route_weights, gate_weight, up_weight, down_weight):
    devices_wide = lax.axis_size("expert")
    groups = lax.axis_size("tensor")
    experts = devices_wide // 2
    tok_count, per_token = expert_ids.shape
    width = tokens.shape[1]
    units = gate_weight.shape[1]
    capacity = min(tok_count, tok_count * per_token // experts)
    arrived_count = devices_wide * capacity

    ids = expert_ids.T
    rings, wide = groups // CORES, CORES * width
    gate_up = (gate_weight[0], up_weight[0])
    part = jax.ShapeDtypeStruct((2 * units, wide), BF16)
    whole = pl.BlockSpec(memory_space=pl.ANY)
    packed, across = pl.pallas_call(
        lambda *refs: pack_kernel(2, 2, *refs),
        out_shape=[jax.ShapeDtypeStruct((devices_wide, capacity, width), BF16), part],
        in_specs=[whole] * 4,
        out_specs=[whole] * 2,
        scratch_shapes=[
            pltpu.VMEM(ids.shape, jnp.int32),
            pltpu.VMEM(tokens.shape, BF16),
            pltpu.VMEM((devices_wide, capacity, width), BF16),
            pltpu.VMEM(part.shape, BF16),
            pltpu.SemaphoreType.DMA((2,)),
            pltpu.SemaphoreType.DMA((2,)),
            pltpu.SemaphoreType.DMA((2,)),
        ],
        name="pack",
    )(ids, tokens, *gate_up)
    mix = pl.pallas_call(
        lambda *refs: mix_kernel(capacity, 1, *refs),
        out_shape=jax.ShapeDtypeStruct((experts * capacity, tok_count), F32),
        compiler_params=pltpu.CompilerParams(vmem_limit_bytes=VMEM_BYTES),
        name="mix",
    )(ids, route_weights.T)

    ahead, behind = cut([("up", 1), ("up", 3)], *gate_up, down_weight[0], wide)
    pieces = [("down", ring) for ring in (1, 2, 3)] + [("up", 0), ("down", 0)]
    *down, own, down_own = cut(pieces, *gate_up, down_weight[0], wide)
    blocks = [own, ahead, across, behind]
    for ring in range(1, rings):
        blocks[ring] = lax.ppermute(
            blocks[ring], "tensor", shift_pairs(groups, ring, 0)
        )
    arrived = lax.all_to_all(packed, "expert", 0, 0, tiled=True)
    arrived = arrived.reshape(arrived_count, width)
    arrived, mix = lax.optimization_barrier((arrived, mix))
    down_near, down_far = down_columns([down_own, *down], width, groups)

    partner = lax.ppermute(arrived, "tensor", shift_pairs(groups, 0, 1))
    near = pl.pallas_call(
        near_kernel,
        out_shape=jax.ShapeDtypeStruct((rings, 2 * units, arrived_count), F32),
        compiler_params=pltpu.CompilerParams(vmem_limit_bytes=VMEM_BYTES),
        cost_estimate=pl.CostEstimate(flops=10**9, bytes_accessed=10**6, transcendentals=0),
        name="near",
    )(arrived, *blocks)
    partial = pl.pallas_call(
        far_kernel,
        out_shape=jax.ShapeDtypeStruct((rings, 2 * units, arrived_count), BF16),
        compiler_params=pltpu.CompilerParams(vmem_limit_bytes=VMEM_BYTES),
        name="far",
    )(partner, near, *blocks)
    same_core = [list(range(core, groups, CORES)) for core in range(CORES)]
    partial = lax.all_to_all(
        partial, "tensor", 0, 0, axis_index_groups=same_core, tiled=True
    )
    hidden = pl.pallas_call(
        hidden_kernel,
        out_shape=jax.ShapeDtypeStruct((groups, units, arrived_count), BF16),
        compiler_params=pltpu.CompilerParams(vmem_limit_bytes=VMEM_BYTES),
        name="hidden",
    )(partial)
    hidden = lax.all_to_all(hidden, "tensor", 0, 0, tiled=True)
    slots = capacity // 2
    kept, given = pl.pallas_call(
        down_kernel,
        out_shape=[jax.ShapeDtypeStruct((devices_wide, slots, width), BF16)] * 2,
        scratch_shapes=[
            pltpu.VMEM((2, groups // 2 * units, arrived_count), BF16),
            pltpu.VMEM((devices_wide, capacity, width), F32),
        ],
        compiler_params=pltpu.CompilerParams(vmem_limit_bytes=VMEM_BYTES),
        name="down",
    )(hidden, down_near, down_far)
    pairs = [(i, i + 1 - 2 * (i % 2)) for i in range(devices_wide)]
    taken = lax.ppermute(given, "expert", pairs)
    both = (kept.astype(F32) + taken.astype(F32)).astype(BF16)
    returned = lax.all_to_all(both, "expert", 0, 0, tiled=True)
    returned = returned.reshape(devices_wide * slots, width)
    return pl.pallas_call(
        combine_kernel,
        out_shape=jax.ShapeDtypeStruct((tok_count, width), BF16),
        compiler_params=pltpu.CompilerParams(vmem_limit_bytes=VMEM_BYTES),
        name="combine",
    )(mix, returned)


def solution(mesh):
    placed = (
        P("expert", "tensor"),
        P("expert", None),
        P("expert", None),
        P("expert", "tensor", None),
        P("expert", "tensor", None),
        P("expert", "tensor", None),
    )
    def step(*args):
        return body(*args)

    step = jax.shard_map(
        step, mesh=mesh, in_specs=placed, out_specs=P("expert", "tensor"), check_vma=False
    )
    return step
```

profile of v0, /device:TPU:6, one launch (start us, length us, event | category | flops | bytes accessed | tf_op | source)
XLA Modules:
  0.0 131.5 jit_solution(2868966734516848583)
XLA Ops:
  0.0 2.2 %pack.1 = (bf16[64,4,896]{2,1,0:T(4,128)(2,1)}, bf16[128,1792]{1,0:T(8,128)(2,1)}) custom-call(s32[8,16]{1,0:T(8,128)} %bitcast.5, bf16[16,896]{1,0:T(8,128)(2,1)} %refs_1_.1, bf16[64,7168]{1,0:T(8,128)(2,1)} %bitcast.8, bf16[64,7168]{1,0:T(8,128)(2,1)} %bitcast.11), custom_call_target="tpu_custom_call" | custom-call | tf_op jit(solution)/shard_map/pack/pallas_call | solution.py:238
  2.2 18.8 %all-to-all-start = ((bf16[64,4,896]{2,1,0:T(4,128)(2,1)}), bf16[64,4,896]{2,1,0:T(4,128)(2,1)S(1)}, u32[]{:S(2)}, u32[]{:S(2)}) async-start(bf16[64,4,896]{2,1,0:T(4,128)(2,1)} %get-tuple-element.20), calls=%async_computation | async-start | bytes 917504 | tf_op jit(solution)/shard_map/all_to_all | solution.py:269
  21.0 2.4 %cut.2 = (bf16[64,1792]{1,0:T(8,128)(2,1)}, bf16[64,1792]{1,0:T(8,128)(2,1)}, bf16[64,1792]{1,0:T(8,128)(2,1)}, bf16[128,1792]{1,0:T(8,128)(2,1)}, bf16[64,1792]{1,0:T(8,128)(2,1)}) custom-call(bf16[64,7168]{1,0:T(8,128)(2,1)} %bitcast.9, bf16[64,7168]{1,0:T(8,128)(2,1)} %bitcast.12, bf16[64,7168]{1,0:T(8,128)(2,1)} %bitcast.14), custom_call_target="tpu_custom_call" | custom-call | tf_op jit(solution)/shard_map/cut/pallas_call | solution.py:130
  23.4 3.5 %collective-permute-start.4 = (bf16[64,1792]{1,0:T(8,128)(2,1)}, bf16[64,1792]{1,0:T(8,128)(2,1)S(1)}, u32[]{:S(2)}, u32[]{:S(2)}) collective-permute-start(bf16[64,1792]{1,0:T(8,128)(2,1)} %get-tuple-element.28), channel_id=1, source_target_pairs={{0,2},{1,3},{2,4},{3,5},{4,6},{5,7},{6,0},{7,1},{8,10},{9,11},{10,... | collective-permute-start | bytes 688136 | tf_op jit(solution)/shard_map/ppermute | solution.py:193
  26.9 4.8 %collective-permute-start.5 = (bf16[64,1792]{1,0:T(8,128)(2,1)}, bf16[64,1792]{1,0:T(8,128)(2,1)S(1)}, u32[]{:S(2)}, u32[]{:S(2)}) collective-permute-start(bf16[64,1792]{1,0:T(8,128)(2,1)} %get-tuple-element.29), channel_id=1, source_target_pairs={{0,4},{1,5},{2,6},{3,7},{4,0},{5,1},{6,2},{7,3},{8,12},{9,13},{10,... | collective-permute-start | bytes 688136 | tf_op jit(solution)/shard_map/ppermute | solution.py:193
  31.7 2.5 %collective-permute-start.2 = (bf16[128,1792]{1,0:T(8,128)(2,1)}, bf16[128,1792]{1,0:T(8,128)(2,1)S(1)}, u32[]{:S(2)}, u32[]{:S(2)}) collective-permute-start(bf16[128,1792]{1,0:T(8,128)(2,1)} %get-tuple-element.25), channel_id=1, source_target_pairs={{0,4},{1,5},{2,6},{3,7},{4,0},{5,1},{6,2},{7,3},{8,12},{9,13},{10,... | collective-permute-start | bytes 1376264 | tf_op jit(solution)/shard_map/ppermute | solution.py:266
  34.2 0.0 copy-start.3
  34.2 2.1 %cut.3 = (bf16[128,1792]{1,0:T(8,128)(2,1)}, bf16[128,1792]{1,0:T(8,128)(2,1)}) custom-call(bf16[64,7168]{1,0:T(8,128)(2,1)} %bitcast.10, bf16[64,7168]{1,0:T(8,128)(2,1)} %bitcast.13, bf16[64,7168]{1,0:T(8,128)(2,1)} %bitcast.15), custom_call_target="tpu_custom_call" | custom-call | tf_op jit(solution)/shard_map/cut/pallas_call | solution.py:130
  36.4 0.0 copy-start.2
  36.4 3.5 %collective-permute-start.1 = (bf16[128,1792]{1,0:T(8,128)(2,1)}, bf16[128,1792]{1,0:T(8,128)(2,1)S(1)}, u32[]{:S(2)}, u32[]{:S(2)}) collective-permute-start(bf16[128,1792]{1,0:T(8,128)(2,1)} %get-tuple-element.24), channel_id=1, source_target_pairs={{0,2},{1,3},{2,4},{3,5},{4,6},{5,7},{6,0},{7,1},{8,10},{9,11},{10,... | collective-permute-start | bytes 1376264 | tf_op jit(solution)/shard_map/ppermute | solution.py:266
  39.9 3.6 %collective-permute-start.3 = (bf16[128,1792]{1,0:T(8,128)(2,1)}, bf16[128,1792]{1,0:T(8,128)(2,1)S(1)}, u32[]{:S(2)}, u32[]{:S(2)}) collective-permute-start(bf16[128,1792]{1,0:T(8,128)(2,1)} %get-tuple-element.26), channel_id=1, source_target_pairs={{0,6},{1,7},{2,0},{3,1},{4,2},{5,3},{6,4},{7,5},{8,14},{9,15},{10,... | collective-permute-start | bytes 1376264 | tf_op jit(solution)/shard_map/ppermute | solution.py:266
  43.5 0.0 copy-done.3
  43.5 0.0 copy-done.2
  43.5 0.2 mix.1.mix_ref
  43.7 0.0 copy-start.4
  43.7 0.0 copy-start.1
  43.7 6.1 %all-to-all-done = bf16[64,4,896]{2,1,0:T(4,128)(2,1)S(1)} async-done(((bf16[64,4,896]{2,1,0:T(4,128)(2,1)}), bf16[64,4,896]{2,1,0:T(4,128)(2,1)S(1)}, u32[]{:S(2)}, u32[]{:S(2)}) %all-to-all-start) | async-done | bytes 458784 | tf_op jit(solution)/shard_map/all_to_all | solution.py:269
  49.8 0.1 reshape.6.rows_ref
  49.9 0.0 collective-permute-done.4.refs_1_
  49.9 1.9 %collective-permute-start = (bf16[256,896]{1,0:T(8,128)(2,1)S(1)}, bf16[256,896]{1,0:T(8,128)(2,1)S(1)}, u32[]{:S(2)}, u32[]{:S(2)}) collective-permute-start(bf16[256,896]{1,0:T(8,128)(2,1)S(1)} %reshape.6.rows_ref), channel_id=1, source_target_pairs={{0,1},{1,0},{2,3},{3,2},{4,5},{5,4},{6,7},{7,6},{8,9},{9,8},{10,11... | collective-permute-start | bytes 1376264 | tf_op jit(solution)/shard_map/ppermute | solution.py:274
  51.8 0.0 collective-permute-done.5.refs_2_
  51.9 0.0 copy-done.4
  51.9 4.9 %collective-permute-start.6 = (bf16[64,1792]{1,0:T(8,128)(2,1)S(1)}, bf16[64,1792]{1,0:T(8,128)(2,1)S(1)}, u32[]{:S(2)}, u32[]{:S(2)}) collective-permute-start(bf16[64,1792]{1,0:T(8,128)(2,1)S(1)} %copy-done.4), channel_id=1, source_target_pairs={{0,6},{1,7},{2,0},{3,1},{4,2},{5,3},{6,4},{7,5},{8,14},{9,15},{10,... | collective-permute-start | bytes 688136 | tf_op jit(solution)/shard_map/ppermute | solution.py:193
  56.8 5.5 %collective-permute-done.6.refs_3_ = bf16[64,1792]{1,0:T(8,128)(2,1)S(1)} collective-permute-done((bf16[64,1792]{1,0:T(8,128)(2,1)S(1)}, bf16[64,1792]{1,0:T(8,128)(2,1)S(1)}, u32[]{:S(2)}, u32[]{:S(2)}) %collective-permute-start.6) | collective-permute-done | bytes 229408 | tf_op jit(solution)/shard_map/ppermute | solution.py:193
  62.3 0.0 copy-done.1
  62.3 0.0 copy-start
  62.3 0.1 core_cut.1
  62.4 2.1 %collective-permute-start.7 = (bf16[256,896]{1,0:T(8,128)(2,1)S(1)}, bf16[256,896]{1,0:T(8,128)(2,1)S(1)}, u32[]{:S(2)}, u32[]{:S(2)}) collective-permute-start(bf16[256,896]{1,0:T(8,128)(2,1)S(1)} %get-tuple-element.32), channel_id=1, source_target_pairs={{0,1},{1,0},{2,3},{3,2},{4,5},{5,4},{6,7},{7,6},{8,9},{9,8},{10,11... | collective-permute-start | bytes 1376264 | tf_op jit(solution)/shard_map/ppermute | solution.py:202
  64.4 0.0 collective-permute-done.2.refs_2_
  64.5 0.0 collective-permute-done.1.refs_1_
  64.5 0.0 collective-permute-done.3.refs_3_
  64.5 0.0 copy-done
  64.5 0.7 near.1.near_ref
  65.2 0.0 collective-permute-done.rows_ref
  65.2 0.7 far.1
  66.0 12.1 %all_to_all.20.partial_ref = bf16[4,128,256]{2,1,0:T(8,128)(2,1)S(1)} all-to-all(bf16[4,128,256]{2,1,0:T(8,128)(2,1)S(1)} %far.1), channel_id=1, replica_groups={{0,2,4,6},{1,3,5,7},{8,10,12,14},{9,11,13,15},{16,18,20,22},{17,19,21,2..., dimensions={0} | all-to-all | bytes 524288 | tf_op jit(solution)/shard_map/all_to_all | solution.py:289
  78.0 0.7 hidden.1
  78.8 3.4 %all-to-all-start.2 = ((bf16[8,64,256]{2,1,0:T(8,128)(2,1)}), bf16[8,64,256]{2,1,0:T(8,128)(2,1)S(1)}, u32[]{:S(2)}, u32[]{:S(2)}) async-start(bf16[8,64,256]{2,1,0:T(8,128)(2,1)} %hidden.1), calls=%async_computation.2 | async-start | bytes 524288 | tf_op jit(solution)/shard_map/all_to_all | solution.py:298
  82.2 0.0 collective-permute-done.7.far_ref
  82.2 7.4 %all-to-all-done.2.hidden_ref = bf16[8,64,256]{2,1,0:T(8,128)(2,1)S(1)} async-done(((bf16[8,64,256]{2,1,0:T(8,128)(2,1)}), bf16[8,64,256]{2,1,0:T(8,128)(2,1)S(1)}, u32[]{:S(2)}, u32[]{:S(2)}) %all-to-all-start.2) | async-done | bytes 262176 | tf_op jit(solution)/shard_map/all_to_all | solution.py:298
  89.6 0.9 down.1
  90.5 3.0 %collective-permute-start.8 = (bf16[64,2,896]{2,1,0:T(2,128)(2,1)S(1)}, bf16[64,2,896]{2,1,0:T(2,128)(2,1)S(1)}, u32[]{:S(2)}, u32[]{:S(2)}) collective-permute-start(bf16[64,2,896]{2,1,0:T(2,128)(2,1)S(1)} %get-tuple-element.34), channel_id=1, source_target_pairs={{0,8},{8,0},{16,24},{24,16},{32,40},{40,32},{48,56},{56,48},{64,72... | collective-permute-start | bytes 688136 | tf_op jit(solution)/shard_map/ppermute | solution.py:311
  93.5 5.9 %collective-permute-done.8 = bf16[64,2,896]{2,1,0:T(2,128)(2,1)S(1)} collective-permute-done((bf16[64,2,896]{2,1,0:T(2,128)(2,1)S(1)}, bf16[64,2,896]{2,1,0:T(2,128)(2,1)S(1)}, u32[]{:S(2)}, u32[]{:S(2)}) %collective-permute-start.8) | collective-permute-done | bytes 229408 | tf_op jit(solution)/shard_map/ppermute | solution.py:311
  99.4 0.2 add_convert_fusion
  99.6 31.0 %all_to_all.21 = bf16[64,2,896]{2,1,0:T(2,128)(2,1)S(1)} all-to-all(bf16[64,2,896]{2,1,0:T(2,128)(2,1)S(1)} %add_convert_fusion), channel_id=1, replica_groups=mesh['expert'=64,'tensor'=8] {'expert'}, dimensions={0} | all-to-all | bytes 458752 | tf_op jit(solution)/shard_map/all_to_all | solution.py:313
  130.6 0.1 reshape.7.rows_ref
  130.7 0.8 combine.1
Async XLA Ops:
  2.2 47.6 %all-to-all-start = ((bf16[64,4,896]{2,1,0:T(4,128)(2,1)}), bf16[64,4,896]{2,1,0:T(4,128)(2,1)S(1)}, u32[]{:S(2)}, u32[]{:S(2)}) async-start(bf16[64,4,896]{2,1,0:T(4,128)(2,1)} %get-tuple-element.20), calls=%async_computation | async-start | bytes 917504 | tf_op jit(solution)/shard_map/all_to_all | solution.py:269
  23.4 26.5 %collective-permute-start.4 = (bf16[64,1792]{1,0:T(8,128)(2,1)}, bf16[64,1792]{1,0:T(8,128)(2,1)S(1)}, u32[]{:S(2)}, u32[]{:S(2)}) collective-permute-start(bf16[64,1792]{1,0:T(8,128)(2,1)} %get-tuple-element.28), channel_id=1, source_target_pairs={{0,2},{1,3},{2,4},{3,5},{4,6},{5,7},{6,0},{7,1},{8,10},{9,11},{10,... | collective-permute-start | bytes 688136 | tf_op jit(solution)/shard_map/ppermute | solution.py:193
  26.9 25.0 %collective-permute-start.5 = (bf16[64,1792]{1,0:T(8,128)(2,1)}, bf16[64,1792]{1,0:T(8,128)(2,1)S(1)}, u32[]{:S(2)}, u32[]{:S(2)}) collective-permute-start(bf16[64,1792]{1,0:T(8,128)(2,1)} %get-tuple-element.29), channel_id=1, source_target_pairs={{0,4},{1,5},{2,6},{3,7},{4,0},{5,1},{6,2},{7,3},{8,12},{9,13},{10,... | collective-permute-start | bytes 688136 | tf_op jit(solution)/shard_map/ppermute | solution.py:193
  31.7 32.8 %collective-permute-start.2 = (bf16[128,1792]{1,0:T(8,128)(2,1)}, bf16[128,1792]{1,0:T(8,128)(2,1)S(1)}, u32[]{:S(2)}, u32[]{:S(2)}) collective-permute-start(bf16[128,1792]{1,0:T(8,128)(2,1)} %get-tuple-element.25), channel_id=1, source_target_pairs={{0,4},{1,5},{2,6},{3,7},{4,0},{5,1},{6,2},{7,3},{8,12},{9,13},{10,... | collective-permute-start | bytes 1376264 | tf_op jit(solution)/shard_map/ppermute | solution.py:266
  34.2 9.2 %copy-start.3 = (f32[16,8]{0,1:T(8,128)S(1)}, f32[16,8]{0,1:T(8,128)}, u32[]{:S(2)}) copy-start(f32[16,8]{0,1:T(8,128)} %param.8) | copy-start | bytes 1540
  36.4 7.1 %copy-start.2 = (s32[16,8]{0,1:T(8,128)S(1)}, s32[16,8]{0,1:T(8,128)}, u32[]{:S(2)}) copy-start(s32[16,8]{0,1:T(8,128)} %param.7) | copy-start | bytes 1540
  36.4 28.1 %collective-permute-start.1 = (bf16[128,1792]{1,0:T(8,128)(2,1)}, bf16[128,1792]{1,0:T(8,128)(2,1)S(1)}, u32[]{:S(2)}, u32[]{:S(2)}) collective-permute-start(bf16[128,1792]{1,0:T(8,128)(2,1)} %get-tuple-element.24), channel_id=1, source_target_pairs={{0,2},{1,3},{2,4},{3,5},{4,6},{5,7},{6,0},{7,1},{8,10},{9,11},{10,... | collective-permute-start | bytes 1376264 | tf_op jit(solution)/shard_map/ppermute | solution.py:266
  39.9 24.6 %collective-permute-start.3 = (bf16[128,1792]{1,0:T(8,128)(2,1)}, bf16[128,1792]{1,0:T(8,128)(2,1)S(1)}, u32[]{:S(2)}, u32[]{:S(2)}) collective-permute-start(bf16[128,1792]{1,0:T(8,128)(2,1)} %get-tuple-element.26), channel_id=1, source_target_pairs={{0,6},{1,7},{2,0},{3,1},{4,2},{5,3},{6,4},{7,5},{8,14},{9,15},{10,... | collective-permute-start | bytes 1376264 | tf_op jit(solution)/shard_map/ppermute | solution.py:266
  43.7 8.2 %copy-start.4 = (bf16[64,1792]{1,0:T(8,128)(2,1)S(1)}, bf16[64,1792]{1,0:T(8,128)(2,1)}, u32[]{:S(2)}) copy-start(bf16[64,1792]{1,0:T(8,128)(2,1)} %get-tuple-element.30) | copy-start | bytes 688132
  43.7 18.6 %copy-start.1 = (bf16[64,1792]{1,0:T(8,128)(2,1)S(1)}, bf16[64,1792]{1,0:T(8,128)(2,1)}, u32[]{:S(2)}) copy-start(bf16[64,1792]{1,0:T(8,128)(2,1)} %get-tuple-element.27.refs_0_) | copy-start | bytes 688132
  49.9 15.3 %collective-permute-start = (bf16[256,896]{1,0:T(8,128)(2,1)S(1)}, bf16[256,896]{1,0:T(8,128)(2,1)S(1)}, u32[]{:S(2)}, u32[]{:S(2)}) collective-permute-start(bf16[256,896]{1,0:T(8,128)(2,1)S(1)} %reshape.6.rows_ref), channel_id=1, source_target_pairs={{0,1},{1,0},{2,3},{3,2},{4,5},{5,4},{6,7},{7,6},{8,9},{9,8},{10,11... | collective-permute-start | bytes 1376264 | tf_op jit(solution)/shard_map/ppermute | solution.py:274
  51.9 10.4 %collective-permute-start.6 = (bf16[64,1792]{1,0:T(8,128)(2,1)S(1)}, bf16[64,1792]{1,0:T(8,128)(2,1)S(1)}, u32[]{:S(2)}, u32[]{:S(2)}) collective-permute-start(bf16[64,1792]{1,0:T(8,128)(2,1)S(1)} %copy-done.4), channel_id=1, source_target_pairs={{0,6},{1,7},{2,0},{3,1},{4,2},{5,3},{6,4},{7,5},{8,14},{9,15},{10,... | collective-permute-start | bytes 688136 | tf_op jit(solution)/shard_map/ppermute | solution.py:193
  62.3 2.2 %copy-start = (bf16[128,1792]{1,0:T(8,128)(2,1)S(1)}, bf16[128,1792]{1,0:T(8,128)(2,1)}, u32[]{:S(2)}) copy-start(bf16[128,1792]{1,0:T(8,128)(2,1)} %get-tuple-element.23.refs_0_) | copy-start | bytes 1376260
  62.4 19.8 %collective-permute-start.7 = (bf16[256,896]{1,0:T(8,128)(2,1)S(1)}, bf16[256,896]{1,0:T(8,128)(2,1)S(1)}, u32[]{:S(2)}, u32[]{:S(2)}) collective-permute-start(bf16[256,896]{1,0:T(8,128)(2,1)S(1)} %get-tuple-element.32), channel_id=1, source_target_pairs={{0,1},{1,0},{2,3},{3,2},{4,5},{5,4},{6,7},{7,6},{8,9},{9,8},{10,11... | collective-permute-start | bytes 1376264 | tf_op jit(solution)/shard_map/ppermute | solution.py:202
  78.8 10.8 %all-to-all-start.2 = ((bf16[8,64,256]{2,1,0:T(8,128)(2,1)}), bf16[8,64,256]{2,1,0:T(8,128)(2,1)S(1)}, u32[]{:S(2)}, u32[]{:S(2)}) async-start(bf16[8,64,256]{2,1,0:T(8,128)(2,1)} %hidden.1), calls=%async_computation.2 | async-start | bytes 524288 | tf_op jit(solution)/shard_map/all_to_all | solution.py:298
  90.5 8.9 %collective-permute-start.8 = (bf16[64,2,896]{2,1,0:T(2,128)(2,1)S(1)}, bf16[64,2,896]{2,1,0:T(2,128)(2,1)S(1)}, u32[]{:S(2)}, u32[]{:S(2)}) collective-permute-start(bf16[64,2,896]{2,1,0:T(2,128)(2,1)S(1)} %get-tuple-element.34), channel_id=1, source_target_pairs={{0,8},{8,0},{16,24},{24,16},{32,40},{40,32},{48,56},{56,48},{64,72... | collective-permute-start | bytes 688136 | tf_op jit(solution)/shard_map/ppermute | solution.py:311
where the time goes:
time: 132 us
  starting transfers between devices  52 us (39%)
  blocking collectives  43 us (33%)
  waiting for transfers between devices  24.9 us (19%)
  Pallas kernels  10.8 us (8%)
    all_to_all x1, blocking collectives, body(): returned = lax.all_to_all(both, 'expert', 0, 0, tiled=True)  31 us
    all_to_all x1, starting transfers between devices, body(): arrived = lax.all_to_all(packed, 'expert', 0, 0, tiled=True)  18.8 us
    ppermute x3, starting transfers between devices, down_columns(): lax.ppermute(blocks[ring], 'tensor', shift_pairs(groups, ring, 0))  13.2 us
    all_to_all x1, blocking collectives, body(): lax.all_to_all(partial, 'tensor', 0, 0, axis_index_groups=same_core, tile...  12.1 us
    ppermute x3, starting transfers between devices, body(): lax.ppermute(blocks[ring], 'tensor', shift_pairs(groups, ring, 0))  9.59 us
    all_to_all x1, waiting for transfers between devices, body(): hidden = lax.all_to_all(hidden, 'tensor', 0, 0, tiled=True)  7.42 us
    all_to_all x1, waiting for transfers between devices, body(): arrived = lax.all_to_all(packed, 'expert', 0, 0, tiled=True)  6.12 us
    ppermute x1, waiting for transfers between devices, body(): taken = lax.ppermute(given, 'expert', pairs)  5.88 us
  transfers between devices with their start and end apart: 11, of which 4 were waited for; matrix products, arithmetic and copies ran while one was open for 0% of the time, Pallas kernels for 5%

commit v1 on v0

--- a/solution.py
+++ b/solution.py
@@ -158,11 +158,18 @@
 
 
 def far_kernel(rows_ref, near_ref, *refs):
-    *blocks, out_ref = refs
+    *blocks, out_ref, held, given = refs
+    rings = len(blocks)
     chip, core = lax.axis_index("tensor") // CORES, lax.rem(lax.axis_index("tensor"), CORES)
+    writes = []
     for ring, block in enumerate(blocks):
-        source = lax.rem(chip - ring + len(blocks), len(blocks))
-        out_ref[source] = (near_ref[source] + half_product(block, rows_ref, 1 - core)).astype(BF16)
+        source = lax.rem(chip - ring + rings, rings)
+        total = near_ref[source] + half_product(block, rows_ref, 1 - core)
+        held[ring] = total.astype(BF16)
+        writes.append(pltpu.make_async_copy(held.at[ring], out_ref.at[source], given.at[ring]))
+        writes[-1].start()
+    for write in writes:
+        write.wait()
 
 
 def hidden_kernel(partial_ref, out_ref):
@@ -202,7 +209,7 @@
     return near, lax.ppermute(far, "tensor", shift_pairs(groups, 0, 1))
 
 
-def down_kernel(hidden_ref, near_ref, far_ref, keep_ref, give_ref, held, rows):
+def down_kernel(hidden_ref, near_ref, far_ref, keep_ref, give_ref, held):
     groups, units, _ = hidden_ref.shape
     me = lax.axis_index("tensor")
     for core in range(CORES):
@@ -212,12 +219,12 @@
     dims = (((0,), (0,)), ((), ()))
     total = lax.dot_general(held[0], near_ref[...], dims, preferred_element_type=F32)
     total = total + lax.dot_general(held[1], far_ref[...], dims, preferred_element_type=F32)
-    rows[...] = total.reshape(rows.shape)
-    slots = keep_ref.shape[1]
+    peers, slots, width = keep_ref.shape
     half = lax.rem(lax.axis_index("expert"), 2)
+    rows = total.astype(BF16).reshape(peers, 2 * slots, width)
     low, high = rows[:, :slots, :], rows[:, slots:, :]
-    keep_ref[...] = jnp.where(half == 0, low, high).astype(BF16)
-    give_ref[...] = jnp.where(half == 0, high, low).astype(BF16)
+    keep_ref[...] = jnp.where(half == 0, low, high)
+    give_ref[...] = jnp.where(half == 0, high, low)
 
 
 def body(tokens, expert_ids, route_weights, gate_weight, up_weight, down_weight):
@@ -268,7 +275,6 @@
         )
     arrived = lax.all_to_all(packed, "expert", 0, 0, tiled=True)
     arrived = arrived.reshape(arrived_count, width)
-    arrived, mix = lax.optimization_barrier((arrived, mix))
     down_near, down_far = down_columns([down_own, *down], width, groups)
 
     partner = lax.ppermute(arrived, "tensor", shift_pairs(groups, 0, 1))
@@ -282,6 +288,11 @@
     partial = pl.pallas_call(
         far_kernel,
         out_shape=jax.ShapeDtypeStruct((rings, 2 * units, arrived_count), BF16),
+        out_specs=whole,
+        scratch_shapes=[
+            pltpu.VMEM((rings, 2 * units, arrived_count), BF16),
+            pltpu.SemaphoreType.DMA((rings,)),
+        ],
         compiler_params=pltpu.CompilerParams(vmem_limit_bytes=VMEM_BYTES),
         name="far",
     )(partner, near, *blocks)
@@ -295,15 +306,13 @@
         compiler_params=pltpu.CompilerParams(vmem_limit_bytes=VMEM_BYTES),
         name="hidden",
     )(partial)
+    hidden, mix = lax.optimization_barrier((hidden, mix))
     hidden = lax.all_to_all(hidden, "tensor", 0, 0, tiled=True)
     slots = capacity // 2
     kept, given = pl.pallas_call(
         down_kernel,
         out_shape=[jax.ShapeDtypeStruct((devices_wide, slots, width), BF16)] * 2,
-        scratch_shapes=[
-            pltpu.VMEM((2, groups // 2 * units, arrived_count), BF16),
-            pltpu.VMEM((devices_wide, capacity, width), F32),
-        ],
+        scratch_shapes=[pltpu.VMEM((2, groups // 2 * units, arrived_count), BF16)],
         compiler_params=pltpu.CompilerParams(vmem_limit_bytes=VMEM_BYTES),
         name="down",
     )(hidden, down_near, down_far)

time: 132 us -> 137 us (1.038)
  waiting for transfers between devices: 24.9 us -> 35.6 us
  blocking collectives: 43 us -> 33.2 us
  starting transfers between devices: 52 us -> 55.8 us
    all_to_all x1 -> x0, blocking collectives: 12.1 us -> none  [body(): lax.all_to_all(partial, 'tensor', 0, 0, axis_index_groups=same_core, tile...]
    all_to_all x0 -> x1, waiting for transfers between devices: none -> 7.13 us  [body(): lax.all_to_all(partial, 'tensor', 0, 0, axis_index_groups=same_core, tile...]
    all_to_all x0 -> x1, starting transfers between devices: none -> 3.9 us  [body(): lax.all_to_all(partial, 'tensor', 0, 0, axis_index_groups=same_core, tile...]
    ppermute x3, waiting for transfers between devices: 5.51 us -> 8.77 us  [down_columns(): lax.ppermute(blocks[ring], 'tensor', shift_pairs(groups, ring, 0))]
    all_to_all x1, blocking collectives: 31 us -> 33.2 us  [body(): returned = lax.all_to_all(both, 'expert', 0, 0, tiled=True)]
  transfers between devices with their start and end apart: 11 -> 12, of which waited for: 4 -> 5; matrix products, arithmetic and copies ran while one was open for 0% -> 0% of each run, Pallas kernels for 5% -> 6%
where the time goes in v1:
time: 137 us
  starting transfers between devices  55.8 us (41%)
  waiting for transfers between devices  35.6 us (26%)
  blocking collectives  33.2 us (24%)
  Pallas kernels  11.2 us (8%)
    all_to_all x1, blocking collectives, body(): returned = lax.all_to_all(both, 'expert', 0, 0, tiled=True)  33.2 us
    all_to_all x1, starting transfers between devices, body(): arrived = lax.all_to_all(packed, 'expert', 0, 0, tiled=True)  18.8 us
    ppermute x3, starting transfers between devices, down_columns(): lax.ppermute(blocks[ring], 'tensor', shift_pairs(groups, ring, 0))  13.2 us
    ppermute x3, starting transfers between devices, body(): lax.ppermute(blocks[ring], 'tensor', shift_pairs(groups, ring, 0))  9.11 us
    ppermute x3, waiting for transfers between devices, down_columns(): lax.ppermute(blocks[ring], 'tensor', shift_pairs(groups, ring, 0))  8.77 us
    all_to_all x1, waiting for transfers between devices, body(): hidden = lax.all_to_all(hidden, 'tensor', 0, 0, tiled=True)  7.42 us
    all_to_all x1, waiting for transfers between devices, body(): lax.all_to_all(partial, 'tensor', 0, 0, axis_index_groups=same_core, tile...  7.13 us
    all_to_all x1, waiting for transfers between devices, body(): arrived = lax.all_to_all(packed, 'expert', 0, 0, tiled=True)  6.81 us
  transfers between devices with their start and end apart: 12, of which 5 were waited for; matrix products, arithmetic and copies ran while one was open for 0% of the time, Pallas kernels for 6%

profile of v1, /device:TPU:6, one launch (start us, length us, event | category | flops | bytes accessed | tf_op | source)
XLA Modules:
  0.0 136.5 jit_solution(16937386790066208711)
XLA Ops:
  0.0 2.2 %pack.1 = (bf16[64,4,896]{2,1,0:T(4,128)(2,1)}, bf16[128,1792]{1,0:T(8,128)(2,1)}) custom-call(s32[8,16]{1,0:T(8,128)} %bitcast.5, bf16[16,896]{1,0:T(8,128)(2,1)} %refs_1_.1, bf16[64,7168]{1,0:T(8,128)(2,1)} %bitcast.8, bf16[64,7168]{1,0:T(8,128)(2,1)} %bitcast.11), custom_call_target="tpu_custom_call" | custom-call | tf_op jit(solution)/shard_map/pack/pallas_call | solution.py:245
  2.2 18.8 %all-to-all-start = ((bf16[64,4,896]{2,1,0:T(4,128)(2,1)}), bf16[64,4,896]{2,1,0:T(4,128)(2,1)S(1)}, u32[]{:S(2)}, u32[]{:S(2)}) async-start(bf16[64,4,896]{2,1,0:T(4,128)(2,1)} %get-tuple-element.20), calls=%async_computation | async-start | bytes 917504 | tf_op jit(solution)/shard_map/all_to_all | solution.py:276
  21.0 2.4 %cut.2 = (bf16[64,1792]{1,0:T(8,128)(2,1)}, bf16[64,1792]{1,0:T(8,128)(2,1)}, bf16[64,1792]{1,0:T(8,128)(2,1)}, bf16[128,1792]{1,0:T(8,128)(2,1)}, bf16[64,1792]{1,0:T(8,128)(2,1)}) custom-call(bf16[64,7168]{1,0:T(8,128)(2,1)} %bitcast.9, bf16[64,7168]{1,0:T(8,128)(2,1)} %bitcast.12, bf16[64,7168]{1,0:T(8,128)(2,1)} %bitcast.14), custom_call_target="tpu_custom_call" | custom-call | tf_op jit(solution)/shard_map/cut/pallas_call | solution.py:130
  23.4 3.5 %collective-permute-start.4 = (bf16[64,1792]{1,0:T(8,128)(2,1)}, bf16[64,1792]{1,0:T(8,128)(2,1)S(1)}, u32[]{:S(2)}, u32[]{:S(2)}) collective-permute-start(bf16[64,1792]{1,0:T(8,128)(2,1)} %get-tuple-element.28), channel_id=1, source_target_pairs={{0,2},{1,3},{2,4},{3,5},{4,6},{5,7},{6,0},{7,1},{8,10},{9,11},{10,... | collective-permute-start | bytes 688136 | tf_op jit(solution)/shard_map/ppermute | solution.py:200
  26.9 4.8 %collective-permute-start.5 = (bf16[64,1792]{1,0:T(8,128)(2,1)}, bf16[64,1792]{1,0:T(8,128)(2,1)S(1)}, u32[]{:S(2)}, u32[]{:S(2)}) collective-permute-start(bf16[64,1792]{1,0:T(8,128)(2,1)} %get-tuple-element.29), channel_id=1, source_target_pairs={{0,4},{1,5},{2,6},{3,7},{4,0},{5,1},{6,2},{7,3},{8,12},{9,13},{10,... | collective-permute-start | bytes 688136 | tf_op jit(solution)/shard_map/ppermute | solution.py:200
  31.7 2.1 %cut.3 = (bf16[128,1792]{1,0:T(8,128)(2,1)}, bf16[128,1792]{1,0:T(8,128)(2,1)}) custom-call(bf16[64,7168]{1,0:T(8,128)(2,1)} %bitcast.10, bf16[64,7168]{1,0:T(8,128)(2,1)} %bitcast.13, bf16[64,7168]{1,0:T(8,128)(2,1)} %bitcast.15), custom_call_target="tpu_custom_call" | custom-call | tf_op jit(solution)/shard_map/cut/pallas_call | solution.py:130
  33.8 1.9 %collective-permute-start.1 = (bf16[128,1792]{1,0:T(8,128)(2,1)}, bf16[128,1792]{1,0:T(8,128)(2,1)S(1)}, u32[]{:S(2)}, u32[]{:S(2)}) collective-permute-start(bf16[128,1792]{1,0:T(8,128)(2,1)} %get-tuple-element.22), channel_id=1, source_target_pairs={{0,2},{1,3},{2,4},{3,5},{4,6},{5,7},{6,0},{7,1},{8,10},{9,11},{10,... | collective-permute-start | bytes 1376264 | tf_op jit(solution)/shard_map/ppermute | solution.py:273
  35.8 4.7 %collective-permute-start.2 = (bf16[128,1792]{1,0:T(8,128)(2,1)}, bf16[128,1792]{1,0:T(8,128)(2,1)S(1)}, u32[]{:S(2)}, u32[]{:S(2)}) collective-permute-start(bf16[128,1792]{1,0:T(8,128)(2,1)} %get-tuple-element.23), channel_id=1, source_target_pairs={{0,4},{1,5},{2,6},{3,7},{4,0},{5,1},{6,2},{7,3},{8,12},{9,13},{10,... | collective-permute-start | bytes 1376264 | tf_op jit(solution)/shard_map/ppermute | solution.py:273
  40.5 0.0 copy-start.4
  40.5 0.0 copy-start.1
  40.5 2.5 %collective-permute-start.3 = (bf16[128,1792]{1,0:T(8,128)(2,1)}, bf16[128,1792]{1,0:T(8,128)(2,1)S(1)}, u32[]{:S(2)}, u32[]{:S(2)}) collective-permute-start(bf16[128,1792]{1,0:T(8,128)(2,1)} %get-tuple-element.24), channel_id=1, source_target_pairs={{0,6},{1,7},{2,0},{3,1},{4,2},{5,3},{6,4},{7,5},{8,14},{9,15},{10,... | collective-permute-start | bytes 1376264 | tf_op jit(solution)/shard_map/ppermute | solution.py:273
  43.0 6.8 %all-to-all-done = bf16[64,4,896]{2,1,0:T(4,128)(2,1)S(1)} async-done(((bf16[64,4,896]{2,1,0:T(4,128)(2,1)}), bf16[64,4,896]{2,1,0:T(4,128)(2,1)S(1)}, u32[]{:S(2)}, u32[]{:S(2)}) %all-to-all-start) | async-done | bytes 458784 | tf_op jit(solution)/shard_map/all_to_all | solution.py:276
  49.8 0.1 reshape.6.rows_ref
  49.9 0.0 collective-permute-done.4.refs_1_
  49.9 1.9 %collective-permute-start = (bf16[256,896]{1,0:T(8,128)(2,1)S(1)}, bf16[256,896]{1,0:T(8,128)(2,1)S(1)}, u32[]{:S(2)}, u32[]{:S(2)}) collective-permute-start(bf16[256,896]{1,0:T(8,128)(2,1)S(1)} %reshape.6.rows_ref), channel_id=1, source_target_pairs={{0,1},{1,0},{2,3},{3,2},{4,5},{5,4},{6,7},{7,6},{8,9},{9,8},{10,11... | collective-permute-start | bytes 1376264 | tf_op jit(solution)/shard_map/ppermute | solution.py:280
  51.9 0.0 collective-permute-done.5.refs_2_
  51.9 0.0 copy-done.4
  51.9 4.9 %collective-permute-start.6 = (bf16[64,1792]{1,0:T(8,128)(2,1)S(1)}, bf16[64,1792]{1,0:T(8,128)(2,1)S(1)}, u32[]{:S(2)}, u32[]{:S(2)}) collective-permute-start(bf16[64,1792]{1,0:T(8,128)(2,1)S(1)} %copy-done.4), channel_id=1, source_target_pairs={{0,6},{1,7},{2,0},{3,1},{4,2},{5,3},{6,4},{7,5},{8,14},{9,15},{10,... | collective-permute-start | bytes 688136 | tf_op jit(solution)/shard_map/ppermute | solution.py:200
  56.8 8.8 %collective-permute-done.6.refs_3_ = bf16[64,1792]{1,0:T(8,128)(2,1)S(1)} collective-permute-done((bf16[64,1792]{1,0:T(8,128)(2,1)S(1)}, bf16[64,1792]{1,0:T(8,128)(2,1)S(1)}, u32[]{:S(2)}, u32[]{:S(2)}) %collective-permute-start.6) | collective-permute-done | bytes 229408 | tf_op jit(solution)/shard_map/ppermute | solution.py:200
  65.6 0.0 copy-done.1
  65.6 0.0 copy-start
  65.6 0.1 core_cut.1
  65.7 2.1 %collective-permute-start.7 = (bf16[256,896]{1,0:T(8,128)(2,1)S(1)}, bf16[256,896]{1,0:T(8,128)(2,1)S(1)}, u32[]{:S(2)}, u32[]{:S(2)}) collective-permute-start(bf16[256,896]{1,0:T(8,128)(2,1)S(1)} %get-tuple-element.32), channel_id=1, source_target_pairs={{0,1},{1,0},{2,3},{3,2},{4,5},{5,4},{6,7},{7,6},{8,9},{9,8},{10,11... | collective-permute-start | bytes 1376264 | tf_op jit(solution)/shard_map/ppermute | solution.py:209
  67.7 0.0 collective-permute-done.1.refs_1_
  67.7 0.0 collective-permute-done.2.refs_2_
  67.7 0.0 collective-permute-done.3.refs_3_
  67.7 0.0 copy-done
  67.8 0.7 near.1.near_ref
  68.5 0.0 collective-permute-done.rows_ref
  68.5 1.4 %far.1 = bf16[4,128,256]{2,1,0:T(8,128)(2,1)} custom-call(bf16[256,896]{1,0:T(8,128)(2,1)S(1)} %collective-permute-done.rows_ref, f32[4,128,256]{2,1,0:T(8,128)S(1)} %near.1.near_ref, bf16[128,1792]{1,0:T(8,128)(2,1)S(1)} %copy-done, bf16[128,1792]{1,0:T(8,128)(2,1)S(1)} %collective-permute-done.1.refs_1_, ...), custom_call_target="tpu_custom_call" | custom-call | tf_op jit(solution)/shard_map/far/pallas_call | solution.py:288
  69.9 0.0 copy-start.2
  69.9 0.0 copy-start.3
  69.9 3.9 %all-to-all-start.1 = ((bf16[4,128,256]{2,1,0:T(8,128)(2,1)}), bf16[4,128,256]{2,1,0:T(8,128)(2,1)S(1)}, u32[]{:S(2)}, u32[]{:S(2)}) async-start(bf16[4,128,256]{2,1,0:T(8,128)(2,1)} %far.1), calls=%async_computation.1 | async-start | bytes 524288 | tf_op jit(solution)/shard_map/all_to_all | solution.py:300
  73.8 0.0 copy-done.2
  73.8 0.0 copy-done.3
  73.8 0.2 mix.1.mix_ref
  74.0 7.1 %all-to-all-done.1.partial_ref = bf16[4,128,256]{2,1,0:T(8,128)(2,1)S(1)} async-done(((bf16[4,128,256]{2,1,0:T(8,128)(2,1)}), bf16[4,128,256]{2,1,0:T(8,128)(2,1)S(1)}, u32[]{:S(2)}, u32[]{:S(2)}) %all-to-all-start.1) | async-done | bytes 262176 | tf_op jit(solution)/shard_map/all_to_all | solution.py:300
  81.2 0.8 hidden.1
  81.9 3.4 %all-to-all-start.2 = ((bf16[8,64,256]{2,1,0:T(8,128)(2,1)}), bf16[8,64,256]{2,1,0:T(8,128)(2,1)S(1)}, u32[]{:S(2)}, u32[]{:S(2)}) async-start(bf16[8,64,256]{2,1,0:T(8,128)(2,1)} %hidden.1), calls=%async_computation.2 | async-start | bytes 524288 | tf_op jit(solution)/shard_map/all_to_all | solution.py:310
  85.3 0.0 collective-permute-done.7.far_ref
  85.3 7.4 %all-to-all-done.2.hidden_ref = bf16[8,64,256]{2,1,0:T(8,128)(2,1)S(1)} async-done(((bf16[8,64,256]{2,1,0:T(8,128)(2,1)}), bf16[8,64,256]{2,1,0:T(8,128)(2,1)S(1)}, u32[]{:S(2)}, u32[]{:S(2)}) %all-to-all-start.2) | async-done | bytes 262176 | tf_op jit(solution)/shard_map/all_to_all | solution.py:310
  92.8 0.5 down.1
  93.3 3.4 %collective-permute-start.8 = (bf16[64,2,896]{2,1,0:T(2,128)(2,1)S(1)}, bf16[64,2,896]{2,1,0:T(2,128)(2,1)S(1)}, u32[]{:S(2)}, u32[]{:S(2)}) collective-permute-start(bf16[64,2,896]{2,1,0:T(2,128)(2,1)S(1)} %get-tuple-element.34), channel_id=1, source_target_pairs={{0,8},{8,0},{16,24},{24,16},{32,40},{40,32},{48,56},{56,48},{64,72... | collective-permute-start | bytes 688136 | tf_op jit(solution)/shard_map/ppermute | solution.py:320
  96.7 5.5 %collective-permute-done.8 = bf16[64,2,896]{2,1,0:T(2,128)(2,1)S(1)} collective-permute-done((bf16[64,2,896]{2,1,0:T(2,128)(2,1)S(1)}, bf16[64,2,896]{2,1,0:T(2,128)(2,1)S(1)}, u32[]{:S(2)}, u32[]{:S(2)}) %collective-permute-start.8) | collective-permute-done | bytes 229408 | tf_op jit(solution)/shard_map/ppermute | solution.py:320
  102.2 0.2 add_convert_fusion
  102.4 33.2 %all_to_all.20 = bf16[64,2,896]{2,1,0:T(2,128)(2,1)S(1)} all-to-all(bf16[64,2,896]{2,1,0:T(2,128)(2,1)S(1)} %add_convert_fusion), channel_id=1, replica_groups=mesh['expert'=64,'tensor'=8] {'expert'}, dimensions={0} | all-to-all | bytes 458752 | tf_op jit(solution)/shard_map/all_to_all | solution.py:322
  135.6 0.1 reshape.7.rows_ref
  135.7 0.8 combine.1
Async XLA Ops:
  2.2 47.6 %all-to-all-start = ((bf16[64,4,896]{2,1,0:T(4,128)(2,1)}), bf16[64,4,896]{2,1,0:T(4,128)(2,1)S(1)}, u32[]{:S(2)}, u32[]{:S(2)}) async-start(bf16[64,4,896]{2,1,0:T(4,128)(2,1)} %get-tuple-element.20), calls=%async_computation | async-start | bytes 917504 | tf_op jit(solution)/shard_map/all_to_all | solution.py:276
  23.4 26.5 %collective-permute-start.4 = (bf16[64,1792]{1,0:T(8,128)(2,1)}, bf16[64,1792]{1,0:T(8,128)(2,1)S(1)}, u32[]{:S(2)}, u32[]{:S(2)}) collective-permute-start(bf16[64,1792]{1,0:T(8,128)(2,1)} %get-tuple-element.28), channel_id=1, source_target_pairs={{0,2},{1,3},{2,4},{3,5},{4,6},{5,7},{6,0},{7,1},{8,10},{9,11},{10,... | collective-permute-start | bytes 688136 | tf_op jit(solution)/shard_map/ppermute | solution.py:200
  26.9 25.0 %collective-permute-start.5 = (bf16[64,1792]{1,0:T(8,128)(2,1)}, bf16[64,1792]{1,0:T(8,128)(2,1)S(1)}, u32[]{:S(2)}, u32[]{:S(2)}) collective-permute-start(bf16[64,1792]{1,0:T(8,128)(2,1)} %get-tuple-element.29), channel_id=1, source_target_pairs={{0,4},{1,5},{2,6},{3,7},{4,0},{5,1},{6,2},{7,3},{8,12},{9,13},{10,... | collective-permute-start | bytes 688136 | tf_op jit(solution)/shard_map/ppermute | solution.py:200
  33.8 33.9 %collective-permute-start.1 = (bf16[128,1792]{1,0:T(8,128)(2,1)}, bf16[128,1792]{1,0:T(8,128)(2,1)S(1)}, u32[]{:S(2)}, u32[]{:S(2)}) collective-permute-start(bf16[128,1792]{1,0:T(8,128)(2,1)} %get-tuple-element.22), channel_id=1, source_target_pairs={{0,2},{1,3},{2,4},{3,5},{4,6},{5,7},{6,0},{7,1},{8,10},{9,11},{10,... | collective-permute-start | bytes 1376264 | tf_op jit(solution)/shard_map/ppermute | solution.py:273
  35.8 32.0 %collective-permute-start.2 = (bf16[128,1792]{1,0:T(8,128)(2,1)}, bf16[128,1792]{1,0:T(8,128)(2,1)S(1)}, u32[]{:S(2)}, u32[]{:S(2)}) collective-permute-start(bf16[128,1792]{1,0:T(8,128)(2,1)} %get-tuple-element.23), channel_id=1, source_target_pairs={{0,4},{1,5},{2,6},{3,7},{4,0},{5,1},{6,2},{7,3},{8,12},{9,13},{10,... | collective-permute-start | bytes 1376264 | tf_op jit(solution)/shard_map/ppermute | solution.py:273
  40.5 11.4 %copy-start.4 = (bf16[64,1792]{1,0:T(8,128)(2,1)S(1)}, bf16[64,1792]{1,0:T(8,128)(2,1)}, u32[]{:S(2)}) copy-start(bf16[64,1792]{1,0:T(8,128)(2,1)} %get-tuple-element.30) | copy-start | bytes 688132
  40.5 25.1 %copy-start.1 = (bf16[64,1792]{1,0:T(8,128)(2,1)S(1)}, bf16[64,1792]{1,0:T(8,128)(2,1)}, u32[]{:S(2)}) copy-start(bf16[64,1792]{1,0:T(8,128)(2,1)} %get-tuple-element.27.refs_0_) | copy-start | bytes 688132
  40.5 27.2 %collective-permute-start.3 = (bf16[128,1792]{1,0:T(8,128)(2,1)}, bf16[128,1792]{1,0:T(8,128)(2,1)S(1)}, u32[]{:S(2)}, u32[]{:S(2)}) collective-permute-start(bf16[128,1792]{1,0:T(8,128)(2,1)} %get-tuple-element.24), channel_id=1, source_target_pairs={{0,6},{1,7},{2,0},{3,1},{4,2},{5,3},{6,4},{7,5},{8,14},{9,15},{10,... | collective-permute-start | bytes 1376264 | tf_op jit(solution)/shard_map/ppermute | solution.py:273
  49.9 18.5 %collective-permute-start = (bf16[256,896]{1,0:T(8,128)(2,1)S(1)}, bf16[256,896]{1,0:T(8,128)(2,1)S(1)}, u32[]{:S(2)}, u32[]{:S(2)}) collective-permute-start(bf16[256,896]{1,0:T(8,128)(2,1)S(1)} %reshape.6.rows_ref), channel_id=1, source_target_pairs={{0,1},{1,0},{2,3},{3,2},{4,5},{5,4},{6,7},{7,6},{8,9},{9,8},{10,11... | collective-permute-start | bytes 1376264 | tf_op jit(solution)/shard_map/ppermute | solution.py:280
  51.9 13.7 %collective-permute-start.6 = (bf16[64,1792]{1,0:T(8,128)(2,1)S(1)}, bf16[64,1792]{1,0:T(8,128)(2,1)S(1)}, u32[]{:S(2)}, u32[]{:S(2)}) collective-permute-start(bf16[64,1792]{1,0:T(8,128)(2,1)S(1)} %copy-done.4), channel_id=1, source_target_pairs={{0,6},{1,7},{2,0},{3,1},{4,2},{5,3},{6,4},{7,5},{8,14},{9,15},{10,... | collective-permute-start | bytes 688136 | tf_op jit(solution)/shard_map/ppermute | solution.py:200
  65.6 2.2 %copy-start = (bf16[128,1792]{1,0:T(8,128)(2,1)S(1)}, bf16[128,1792]{1,0:T(8,128)(2,1)}, u32[]{:S(2)}) copy-start(bf16[128,1792]{1,0:T(8,128)(2,1)} %get-tuple-element.21.refs_0_) | copy-start | bytes 1376260
  65.7 19.7 %collective-permute-start.7 = (bf16[256,896]{1,0:T(8,128)(2,1)S(1)}, bf16[256,896]{1,0:T(8,128)(2,1)S(1)}, u32[]{:S(2)}, u32[]{:S(2)}) collective-permute-start(bf16[256,896]{1,0:T(8,128)(2,1)S(1)} %get-tuple-element.32), channel_id=1, source_target_pairs={{0,1},{1,0},{2,3},{3,2},{4,5},{5,4},{6,7},{7,6},{8,9},{9,8},{10,11... | collective-permute-start | bytes 1376264 | tf_op jit(solution)/shard_map/ppermute | solution.py:209
  69.9 3.9 %copy-start.2 = (s32[16,8]{0,1:T(8,128)S(1)}, s32[16,8]{0,1:T(8,128)}, u32[]{:S(2)}) copy-start(s32[16,8]{0,1:T(8,128)} %param.7) | copy-start | bytes 1540
  69.9 3.9 %copy-start.3 = (f32[16,8]{0,1:T(8,128)S(1)}, f32[16,8]{0,1:T(8,128)}, u32[]{:S(2)}) copy-start(f32[16,8]{0,1:T(8,128)} %param.8) | copy-start | bytes 1540
  69.9 11.2 %all-to-all-start.1 = ((bf16[4,128,256]{2,1,0:T(8,128)(2,1)}), bf16[4,128,256]{2,1,0:T(8,128)(2,1)S(1)}, u32[]{:S(2)}, u32[]{:S(2)}) async-start(bf16[4,128,256]{2,1,0:T(8,128)(2,1)} %far.1), calls=%async_computation.1 | async-start | bytes 524288 | tf_op jit(solution)/shard_map/all_to_all | solution.py:300
  81.9 10.8 %all-to-all-start.2 = ((bf16[8,64,256]{2,1,0:T(8,128)(2,1)}), bf16[8,64,256]{2,1,0:T(8,128)(2,1)S(1)}, u32[]{:S(2)}, u32[]{:S(2)}) async-start(bf16[8,64,256]{2,1,0:T(8,128)(2,1)} %hidden.1), calls=%async_computation.2 | async-start | bytes 524288 | tf_op jit(solution)/shard_map/all_to_all | solution.py:310
  93.3 8.9 %collective-permute-start.8 = (bf16[64,2,896]{2,1,0:T(2,128)(2,1)S(1)}, bf16[64,2,896]{2,1,0:T(2,128)(2,1)S(1)}, u32[]{:S(2)}, u32[]{:S(2)}) collective-permute-start(bf16[64,2,896]{2,1,0:T(2,128)(2,1)S(1)} %get-tuple-element.34), channel_id=1, source_target_pairs={{0,8},{8,0},{16,24},{24,16},{32,40},{40,32},{48,56},{56,48},{64,72... | collective-permute-start | bytes 688136 | tf_op jit(solution)/shard_map/ppermute | solution.py:320

commit v2 on v1

--- a/solution.py
+++ b/solution.py
@@ -24,7 +24,9 @@
     return jnp.where((hit > 0.5) & (earlier == rank), 1.0, 0.0), expert
 
 
-def pack_kernel(copies, ring, ids_ref, tok_ref, gate_ref, up_ref, out_ref, block_ref, *refs):
+def pack_kernel(copies, ring, ids_ref, tok_ref, *refs):
+    *weights, out_ref, block_ref = refs[:5]
+    refs = refs[5:]
     ids, tok, packed, held, taken, given, small = refs
     fetches = [
         pltpu.make_async_copy(ids_ref, ids, small.at[0]),
@@ -32,7 +34,7 @@
     ]
     for fetch in fetches:
         fetch.start()
-    reads = cut_reads(ring, (gate_ref, up_ref), held, taken)
+    reads = cut_reads(ring, weights, held, taken)
     peers, capacity, width = packed.shape
     for fetch in fetches:
         fetch.wait()
@@ -106,46 +108,49 @@
     return reads
 
 
-def cut_kernel(pieces, gate_ref, up_ref, down_ref, *refs):
-    outs, refs = refs[: len(pieces)], refs[len(pieces) :]
-    held, (taken, given) = refs[:-2], refs[-2:]
-    reads = []
-    for place, (which, ring) in enumerate(pieces):
-        weights = (gate_ref, up_ref) if which == "up" else (down_ref,)
-        reads.append(cut_reads(ring, weights, held[place], taken.at[place]))
+def cut_kernel(rings, *refs):
+    *refs, held, taken, given = refs
+    weights, outs = refs[: -len(rings)], refs[-len(rings) :]
+    reads = [
+        cut_reads(ring, weights, held.at[place], taken.at[place])
+        for place, ring in enumerate(rings)
+    ]
     writes = []
     for place, out in enumerate(outs):
         for read in reads[place]:
             read.wait()
-        writes.append(pltpu.make_async_copy(held[place], out, given.at[place]))
+        writes.append(pltpu.make_async_copy(held.at[place], out, given.at[place]))
         writes[-1].start()
     for write in writes:
         write.wait()
 
 
-def cut(pieces, gate, up, down, wide):
-    units = gate.shape[0]
-    shapes = [(2 * units if which == "up" else units, wide) for which, _ in pieces]
+def cut(rings, weights, wide):
+    parts = len(weights)
+    shape = jax.ShapeDtypeStruct((parts * weights[0].shape[0], wide), BF16)
     whole = pl.BlockSpec(memory_space=pl.ANY)
     return pl.pallas_call(
-        lambda *refs: cut_kernel(pieces, *refs),
-        out_shape=[jax.ShapeDtypeStruct(shape, BF16) for shape in shapes],
-        in_specs=[whole] * 3,
-        out_specs=[whole] * len(pieces),
-        scratch_shapes=[pltpu.VMEM(shape, BF16) for shape in shapes]
-        + [
-            pltpu.SemaphoreType.DMA((len(pieces), 2)),
-            pltpu.SemaphoreType.DMA((len(pieces),)),
+        lambda *refs: cut_kernel(rings, *refs),
+        out_shape=[shape] * len(rings),
+        in_specs=[whole] * parts,
+        out_specs=[whole] * len(rings),
+        scratch_shapes=[
+            pltpu.VMEM((len(rings), *shape.shape), BF16),
+            pltpu.SemaphoreType.DMA((len(rings), parts)),
+            pltpu.SemaphoreType.DMA((len(rings),)),
         ],
         name="cut",
-    )(gate, up, down)
-
-
-def half_product(block_ref, rows_ref, half):
+    )(*weights)
+
+
+def half_product(block_ref, rows_ref, half, rows):
     width = rows_ref.shape[1]
     cols = pl.ds(pl.multiple_of(half * width, 128), width)
     return lax.dot_general(
-        block_ref[:, cols], rows_ref[...], (((1,), (1,)), ((), ())), preferred_element_type=F32
+        block_ref[:rows, cols],
+        rows_ref[...],
+        (((1,), (1,)), ((), ())),
+        preferred_element_type=F32,
     )
 
 
@@ -154,7 +159,7 @@
     chip, core = lax.axis_index("tensor") // CORES, lax.rem(lax.axis_index("tensor"), CORES)
     for ring, block in enumerate(blocks):
         source = lax.rem(chip - ring + len(blocks), len(blocks))
-        out_ref[source] = half_product(block, rows_ref, core)
+        out_ref[source] = half_product(block, rows_ref, core, out_ref.shape[1])
 
 
 def far_kernel(rows_ref, near_ref, *refs):
@@ -164,7 +169,9 @@
     writes = []
     for ring, block in enumerate(blocks):
         source = lax.rem(chip - ring + rings, rings)
-        total = near_ref[source] + half_product(block, rows_ref, 1 - core)
+        total = near_ref[source] + half_product(
+            block, rows_ref, 1 - core, near_ref.shape[1]
+        )
         held[ring] = total.astype(BF16)
         writes.append(pltpu.make_async_copy(held.at[ring], out_ref.at[source], given.at[ring]))
         writes[-1].start()
@@ -186,20 +193,18 @@
 def core_cut_kernel(*refs):
     *blocks, near_ref, far_ref = refs
     core = lax.rem(lax.axis_index("tensor"), CORES)
-    units = blocks[0].shape[0]
+    units = near_ref.shape[0] // len(blocks)
     width = near_ref.shape[1]
+    own, other = pl.multiple_of(core * width, 128), pl.multiple_of((1 - core) * width, 128)
     for ring, block in enumerate(blocks):
         rows = pl.ds(ring * units, units)
-        near_ref[rows, :] = block[:, pl.ds(pl.multiple_of(core * width, 128), width)]
-        far_ref[rows, :] = block[:, pl.ds(pl.multiple_of((1 - core) * width, 128), width)]
+        last = pl.ds(block.shape[0] - units, units)
+        near_ref[rows, :] = block[last, pl.ds(own, width)]
+        far_ref[rows, :] = block[last, pl.ds(other, width)]
 
 
 def down_columns(blocks, width, groups):
     units, rings = blocks[0].shape[0], len(blocks)
-    for ring in range(1, rings):
-        blocks[ring] = lax.ppermute(
-            blocks[ring], "tensor", shift_pairs(groups, ring, 0)
-        )
     near, far = pl.pallas_call(
         core_cut_kernel,
         out_shape=[jax.ShapeDtypeStruct((rings * units, width), BF16)] * 2,
@@ -221,10 +226,10 @@
     total = total + lax.dot_general(held[1], far_ref[...], dims, preferred_element_type=F32)
     peers, slots, width = keep_ref.shape
     half = lax.rem(lax.axis_index("expert"), 2)
-    rows = total.astype(BF16).reshape(peers, 2 * slots, width)
-    low, high = rows[:, :slots, :], rows[:, slots:, :]
-    keep_ref[...] = jnp.where(half == 0, low, high)
-    give_ref[...] = jnp.where(half == 0, high, low)
+    rows = total.astype(BF16).reshape(peers, 2, slots, width)
+    even, odd = rows[:, 0], rows[:, 1]
+    keep_ref[...] = jnp.where(half == 0, even, odd)
+    give_ref[...] = jnp.where(half == 0, odd, even)
 
 
 def body(tokens, expert_ids, route_weights, gate_weight, up_weight, down_weight):
@@ -239,25 +244,25 @@
 
     ids = expert_ids.T
     rings, wide = groups // CORES, CORES * width
-    gate_up = (gate_weight[0], up_weight[0])
-    part = jax.ShapeDtypeStruct((2 * units, wide), BF16)
+    weights = (gate_weight[0], up_weight[0], down_weight[0])
+    part = jax.ShapeDtypeStruct((3 * units, wide), BF16)
     whole = pl.BlockSpec(memory_space=pl.ANY)
     packed, across = pl.pallas_call(
         lambda *refs: pack_kernel(2, 2, *refs),
         out_shape=[jax.ShapeDtypeStruct((devices_wide, capacity, width), BF16), part],
-        in_specs=[whole] * 4,
+        in_specs=[whole] * 5,
         out_specs=[whole] * 2,
         scratch_shapes=[
             pltpu.VMEM(ids.shape, jnp.int32),
             pltpu.VMEM(tokens.shape, BF16),
             pltpu.VMEM((devices_wide, capacity, width), BF16),
             pltpu.VMEM(part.shape, BF16),
-            pltpu.SemaphoreType.DMA((2,)),
+            pltpu.SemaphoreType.DMA((3,)),
             pltpu.SemaphoreType.DMA((2,)),
             pltpu.SemaphoreType.DMA((2,)),
         ],
         name="pack",
-    )(ids, tokens, *gate_up)
+    )(ids, tokens, *weights)
     mix = pl.pallas_call(
         lambda *refs: mix_kernel(capacity, 1, *refs),
         out_shape=jax.ShapeDtypeStruct((experts * capacity, tok_count), F32),
@@ -265,9 +270,9 @@
         name="mix",
     )(ids, route_weights.T)
 
-    ahead, behind = cut([("up", 1), ("up", 3)], *gate_up, down_weight[0], wide)
-    pieces = [("down", ring) for ring in (1, 2, 3)] + [("up", 0), ("down", 0)]
-    *down, own, down_own = cut(pieces, *gate_up, down_weight[0], wide)
+    ahead, behind = cut((1, 3), weights, wide)
+    (own,) = cut((0,), weights[:2], wide)
+    (own_down,) = cut((0,), weights[2:], wide)
     blocks = [own, ahead, across, behind]
     for ring in range(1, rings):
         blocks[ring] = lax.ppermute(
@@ -275,7 +280,7 @@
         )
     arrived = lax.all_to_all(packed, "expert", 0, 0, tiled=True)
     arrived = arrived.reshape(arrived_count, width)
-    down_near, down_far = down_columns([down_own, *down], width, groups)
+    down_near, down_far = down_columns([own_down, *blocks[1:]], width, groups)
 
     partner = lax.ppermute(arrived, "tensor", shift_pairs(groups, 0, 1))
     near = pl.pallas_call(
@@ -308,10 +313,9 @@
     )(partial)
     hidden, mix = lax.optimization_barrier((hidden, mix))
     hidden = lax.all_to_all(hidden, "tensor", 0, 0, tiled=True)
-    slots = capacity // 2
     kept, given = pl.pallas_call(
         down_kernel,
-        out_shape=[jax.ShapeDtypeStruct((devices_wide, slots, width), BF16)] * 2,
+        out_shape=[jax.ShapeDtypeStruct((experts, capacity, width), BF16)] * 2,
         scratch_shapes=[pltpu.VMEM((2, groups // 2 * units, arrived_count), BF16)],
         compiler_params=pltpu.CompilerParams(vmem_limit_bytes=VMEM_BYTES),
         name="down",
@@ -319,8 +323,11 @@
     pairs = [(i, i + 1 - 2 * (i % 2)) for i in range(devices_wide)]
     taken = lax.ppermute(given, "expert", pairs)
     both = (kept.astype(F32) + taken.astype(F32)).astype(BF16)
-    returned = lax.all_to_all(both, "expert", 0, 0, tiled=True)
-    returned = returned.reshape(devices_wide * slots, width)
+    same_half = [list(range(half, devices_wide, 2)) for half in range(2)]
+    returned = lax.all_to_all(
+        both, "expert", 0, 0, axis_index_groups=same_half, tiled=True
+    )
+    returned = returned.reshape(experts * capacity, width)
     return pl.pallas_call(
         combine_kernel,
         out_shape=jax.ShapeDtypeStruct((tok_count, width), BF16),

time: 137 us -> 130 us (0.949); the launches traced: 137 us -> 128 us
  starting transfers between devices: 55.8 us -> 46.2 us
  Pallas kernels: 11.2 us -> 14.4 us
  blocking collectives: 33.2 us -> 30.9 us
  local copies, waits for them, and re-layouts: 0.22 us -> 1.9 us
  waiting for transfers between devices: 35.6 us -> 34.2 us
    ppermute x3 -> x0, starting transfers between devices: 13.2 us -> none  [down_columns(): lax.ppermute(blocks[ring], 'tensor', shift_pairs(groups, ring, 0))]
    ppermute x3 -> x0, waiting for transfers between devices: 8.77 us -> none  [down_columns(): lax.ppermute(blocks[ring], 'tensor', shift_pairs(groups, ring, 0))]
    all_to_all x1, waiting for transfers between devices: 6.81 us -> 14.2 us  [body(): arrived = lax.all_to_all(packed, 'expert', 0, 0, tiled=True)]
    ppermute x3, starting transfers between devices: 9.11 us -> 12.2 us  [body(): lax.ppermute(blocks[ring], 'tensor', shift_pairs(groups, ring, 0))]
    all_to_all x1, blocking collectives: 33.2 us -> 30.9 us  [body(): lax.all_to_all(both, 'expert', 0, 0, axis_index_groups=same_half, tiled=T...]
    pallas_call x3 -> x4, Pallas kernels: 5.03 us -> 6.39 us  [the longest x3 5.9 us: cut(): pl.pallas_call(lambda *refs: cut_kernel(rings, *refs), out_shape=[shape]...]
  transfers between devices with their start and end apart: 12 -> 9, of which waited for: 5 -> 5; matrix products, arithmetic and copies ran while one was open for 0% -> 1% of each run, Pallas kernels for 6% -> 8%
where the time goes in v2:
time: 130 us; the launch traced here: 128 us
  starting transfers between devices  46.2 us (36%)
  waiting for transfers between devices  34.2 us (26%)
  blocking collectives  30.9 us (24%)
  Pallas kernels  14.4 us (11%)
  local copies, waits for them, and re-layouts  1.9 us (1%)
    all_to_all x1, blocking collectives, body(): lax.all_to_all(both, 'expert', 0, 0, axis_index_groups=same_half, tiled=T...  30.9 us
    all_to_all x1, starting transfers between devices, body(): arrived = lax.all_to_all(packed, 'expert', 0, 0, tiled=True)  18.8 us
    all_to_all x1, waiting for transfers between devices, body(): arrived = lax.all_to_all(packed, 'expert', 0, 0, tiled=True)  14.2 us
    ppermute x3, starting transfers between devices, body(): lax.ppermute(blocks[ring], 'tensor', shift_pairs(groups, ring, 0))  12.2 us
    all_to_all x1, waiting for transfers between devices, body(): hidden = lax.all_to_all(hidden, 'tensor', 0, 0, tiled=True)  7.42 us
    all_to_all x1, waiting for transfers between devices, body(): lax.all_to_all(partial, 'tensor', 0, 0, axis_index_groups=same_core, tile...  6.65 us
    pallas_call x3, Pallas kernels, cut(): pl.pallas_call(lambda *refs: cut_kernel(rings, *refs), out_shape=[shape]...  5.9 us
    ppermute x1, waiting for transfers between devices, body(): taken = lax.ppermute(given, 'expert', pairs)  5.74 us
  transfers between devices with their start and end apart: 9, of which 5 were waited for; matrix products, arithmetic and copies ran while one was open for 1% of the time, Pallas kernels for 8%

profile of v2, /device:TPU:6, one launch (start us, length us, event | category | flops | bytes accessed | tf_op | source)
XLA Modules:
  0.0 128.0 jit_solution(9444146544647923431)
XLA Ops:
  0.0 2.3 %pack.1 = (bf16[64,4,896]{2,1,0:T(4,128)(2,1)}, bf16[192,1792]{1,0:T(8,128)(2,1)}) custom-call(s32[8,16]{1,0:T(8,128)} %bitcast.5, bf16[16,896]{1,0:T(8,128)(2,1)} %refs_1_.1, bf16[64,7168]{1,0:T(8,128)(2,1)} %bitcast.8, bf16[64,7168]{1,0:T(8,128)(2,1)} %bitcast.11, bf16[64,7168]{1,0:T(8,128)(2,1)} %bitcast.14), custom_call_target="tpu_custom_call" | custom-call | tf_op jit(solution)/shard_map/pack/pallas_call | solution.py:250
  2.3 18.8 %all-to-all-start = ((bf16[64,4,896]{2,1,0:T(4,128)(2,1)}), bf16[64,4,896]{2,1,0:T(4,128)(2,1)S(1)}, u32[]{:S(2)}, u32[]{:S(2)}) async-start(bf16[64,4,896]{2,1,0:T(4,128)(2,1)} %get-tuple-element.15), calls=%async_computation | async-start | bytes 917504 | tf_op jit(solution)/shard_map/all_to_all | solution.py:281
  21.1 5.1 %collective-permute-start.2 = (bf16[192,1792]{1,0:T(8,128)(2,1)}, bf16[192,1792]{1,0:T(8,128)(2,1)S(1)}, u32[]{:S(2)}, u32[]{:S(2)}) collective-permute-start(bf16[192,1792]{1,0:T(8,128)(2,1)} %get-tuple-element.17), channel_id=1, source_target_pairs={{0,4},{1,5},{2,6},{3,7},{4,0},{5,1},{6,2},{7,3},{8,12},{9,13},{10,... | collective-permute-start | bytes 2064392 | tf_op jit(solution)/shard_map/ppermute | solution.py:278
  26.2 2.4 %cut.4 = (bf16[192,1792]{1,0:T(8,128)(2,1)}, bf16[192,1792]{1,0:T(8,128)(2,1)}) custom-call(bf16[64,7168]{1,0:T(8,128)(2,1)} %bitcast.9, bf16[64,7168]{1,0:T(8,128)(2,1)} %bitcast.12, bf16[64,7168]{1,0:T(8,128)(2,1)} %bitcast.15), custom_call_target="tpu_custom_call" | custom-call | tf_op jit(solution)/shard_map/cut/pallas_call | solution.py:132
  28.6 2.6 %collective-permute-start.1 = (bf16[192,1792]{1,0:T(8,128)(2,1)}, bf16[192,1792]{1,0:T(8,128)(2,1)S(1)}, u32[]{:S(2)}, u32[]{:S(2)}) collective-permute-start(bf16[192,1792]{1,0:T(8,128)(2,1)} %get-tuple-element.16), channel_id=1, source_target_pairs={{0,2},{1,3},{2,4},{3,5},{4,6},{5,7},{6,0},{7,1},{8,10},{9,11},{10,... | collective-permute-start | bytes 2064392 | tf_op jit(solution)/shard_map/ppermute | solution.py:278
  31.2 4.5 %collective-permute-start.3 = (bf16[192,1792]{1,0:T(8,128)(2,1)}, bf16[192,1792]{1,0:T(8,128)(2,1)S(1)}, u32[]{:S(2)}, u32[]{:S(2)}) collective-permute-start(bf16[192,1792]{1,0:T(8,128)(2,1)} %get-tuple-element.18), channel_id=1, source_target_pairs={{0,6},{1,7},{2,0},{3,1},{4,2},{5,3},{6,4},{7,5},{8,14},{9,15},{10,... | collective-permute-start | bytes 2064392 | tf_op jit(solution)/shard_map/ppermute | solution.py:278
  35.6 14.2 %all-to-all-done = bf16[64,4,896]{2,1,0:T(4,128)(2,1)S(1)} async-done(((bf16[64,4,896]{2,1,0:T(4,128)(2,1)}), bf16[64,4,896]{2,1,0:T(4,128)(2,1)S(1)}, u32[]{:S(2)}, u32[]{:S(2)}) %all-to-all-start) | async-done | bytes 458784 | tf_op jit(solution)/shard_map/all_to_all | solution.py:281
  49.9 0.9 reshape.6.rows_ref
  50.8 1.9 %collective-permute-start = (bf16[256,896]{1,0:T(8,128)(2,1)}, bf16[256,896]{1,0:T(8,128)(2,1)S(1)}, u32[]{:S(2)}, u32[]{:S(2)}) collective-permute-start(bf16[256,896]{1,0:T(8,128)(2,1)} %reshape.6.rows_ref), channel_id=1, source_target_pairs={{0,1},{1,0},{2,3},{3,2},{4,5},{5,4},{6,7},{7,6},{8,9},{9,8},{10,11... | collective-permute-start | bytes 1376264 | tf_op jit(solution)/shard_map/ppermute | solution.py:285
  52.7 1.9 %cut.3.refs_0_ = bf16[128,1792]{1,0:T(8,128)(2,1)} custom-call(bf16[64,7168]{1,0:T(8,128)(2,1)} %bitcast.10, bf16[64,7168]{1,0:T(8,128)(2,1)} %bitcast.13), custom_call_target="tpu_custom_call" | custom-call | tf_op jit(solution)/shard_map/cut/pallas_call | solution.py:132
  54.6 1.7 %cut.5.refs_0_ = bf16[64,1792]{1,0:T(8,128)(2,1)} custom-call(bf16[64,7168]{1,0:T(8,128)(2,1)} %bitcast.16), custom_call_target="tpu_custom_call" | custom-call | tf_op jit(solution)/shard_map/cut/pallas_call | solution.py:132
  56.2 0.0 copy-start
  56.2 0.0 collective-permute-done.2.refs_2_
  56.2 0.0 collective-permute-done.1.refs_1_
  56.2 0.2 collective-permute-done.3.refs_3_
  56.4 0.0 copy-start.1
  56.4 0.9 copy-done.1
  57.4 0.8 core_cut.1
  58.2 2.3 %collective-permute-start.4 = (bf16[256,896]{1,0:T(8,128)(2,1)}, bf16[256,896]{1,0:T(8,128)(2,1)S(1)}, u32[]{:S(2)}, u32[]{:S(2)}) collective-permute-start(bf16[256,896]{1,0:T(8,128)(2,1)} %get-tuple-element.22), channel_id=1, source_target_pairs={{0,1},{1,0},{2,3},{3,2},{4,5},{5,4},{6,7},{7,6},{8,9},{9,8},{10,11... | collective-permute-start | bytes 1376264 | tf_op jit(solution)/shard_map/ppermute | solution.py:214
  60.5 0.0 copy-done
  60.5 1.7 %near.1.near_ref = f32[4,128,256]{2,1,0:T(8,128)S(1)} custom-call(bf16[256,896]{1,0:T(8,128)(2,1)} %reshape.6.rows_ref, bf16[128,1792]{1,0:T(8,128)(2,1)S(1)} %copy-done, bf16[192,1792]{1,0:T(8,128)(2,1)S(1)} %collective-permute-done.1.refs_1_, bf16[192,1792]{1,0:T(8,128)(2,1)S(1)} %collective-permute-done.2.refs_2_, ...), custom_call_target="tpu_custom_call" | custom-call | flops 1000000000 | bytes 1000000 | tf_op jit(solution)/shard_map/near/pallas_call | solution.py:286
  62.2 0.0 collective-permute-done.rows_ref
  62.2 1.4 %far.1 = bf16[4,128,256]{2,1,0:T(8,128)(2,1)} custom-call(bf16[256,896]{1,0:T(8,128)(2,1)S(1)} %collective-permute-done.rows_ref, f32[4,128,256]{2,1,0:T(8,128)S(1)} %near.1.near_ref, bf16[128,1792]{1,0:T(8,128)(2,1)S(1)} %copy-done, bf16[192,1792]{1,0:T(8,128)(2,1)S(1)} %collective-permute-done.1.refs_1_, ...), custom_call_target="tpu_custom_call" | custom-call | tf_op jit(solution)/shard_map/far/pallas_call | solution.py:293
  63.7 0.0 copy-start.2
  63.7 0.0 copy-start.3
  63.7 4.5 %all-to-all-start.1 = ((bf16[4,128,256]{2,1,0:T(8,128)(2,1)}), bf16[4,128,256]{2,1,0:T(8,128)(2,1)S(1)}, u32[]{:S(2)}, u32[]{:S(2)}) async-start(bf16[4,128,256]{2,1,0:T(8,128)(2,1)} %far.1), calls=%async_computation.1 | async-start | bytes 524288 | tf_op jit(solution)/shard_map/all_to_all | solution.py:305
  68.2 0.0 copy-done.2
  68.2 0.0 copy-done.3
  68.2 0.2 mix.1.mix_ref
  68.4 6.6 %all-to-all-done.1.partial_ref = bf16[4,128,256]{2,1,0:T(8,128)(2,1)S(1)} async-done(((bf16[4,128,256]{2,1,0:T(8,128)(2,1)}), bf16[4,128,256]{2,1,0:T(8,128)(2,1)S(1)}, u32[]{:S(2)}, u32[]{:S(2)}) %all-to-all-start.1) | async-done | bytes 262176 | tf_op jit(solution)/shard_map/all_to_all | solution.py:305
  75.0 0.8 hidden.1
  75.8 3.4 %all-to-all-start.2 = ((bf16[8,64,256]{2,1,0:T(8,128)(2,1)}), bf16[8,64,256]{2,1,0:T(8,128)(2,1)S(1)}, u32[]{:S(2)}, u32[]{:S(2)}) async-start(bf16[8,64,256]{2,1,0:T(8,128)(2,1)} %hidden.1), calls=%async_computation.2 | async-start | bytes 524288 | tf_op jit(solution)/shard_map/all_to_all | solution.py:315
  79.2 0.0 collective-permute-done.4.far_ref
  79.2 7.4 %all-to-all-done.2.hidden_ref = bf16[8,64,256]{2,1,0:T(8,128)(2,1)S(1)} async-done(((bf16[8,64,256]{2,1,0:T(8,128)(2,1)}), bf16[8,64,256]{2,1,0:T(8,128)(2,1)S(1)}, u32[]{:S(2)}, u32[]{:S(2)}) %all-to-all-start.2) | async-done | bytes 262176 | tf_op jit(solution)/shard_map/all_to_all | solution.py:315
  86.6 0.5 down.1
  87.1 3.1 %collective-permute-start.5 = (bf16[32,4,896]{2,1,0:T(4,128)(2,1)S(1)}, bf16[32,4,896]{2,1,0:T(4,128)(2,1)S(1)}, u32[]{:S(2)}, u32[]{:S(2)}) collective-permute-start(bf16[32,4,896]{2,1,0:T(4,128)(2,1)S(1)} %get-tuple-element.24), channel_id=1, source_target_pairs={{0,8},{8,0},{16,24},{24,16},{32,40},{40,32},{48,56},{56,48},{64,72... | collective-permute-start | bytes 688136 | tf_op jit(solution)/shard_map/ppermute | solution.py:324
  90.2 5.7 %collective-permute-done.5 = bf16[32,4,896]{2,1,0:T(4,128)(2,1)S(1)} collective-permute-done((bf16[32,4,896]{2,1,0:T(4,128)(2,1)S(1)}, bf16[32,4,896]{2,1,0:T(4,128)(2,1)S(1)}, u32[]{:S(2)}, u32[]{:S(2)}) %collective-permute-start.5) | collective-permute-done | bytes 229408 | tf_op jit(solution)/shard_map/ppermute | solution.py:324
  96.0 0.1 add_convert_fusion
  96.1 30.9 %all_to_all.20 = bf16[32,4,896]{2,1,0:T(4,128)(2,1)S(1)} all-to-all(bf16[32,4,896]{2,1,0:T(4,128)(2,1)S(1)} %add_convert_fusion), channel_id=1, replica_groups={{0,16,32,48,64,80,96,112,128,144,160,176,192,208,224,240,256,272,288,30..., dimensions={0} | all-to-all | bytes 458752 | tf_op jit(solution)/shard_map/all_to_all | solution.py:327
  127.1 0.1 reshape.7.rows_ref
  127.1 0.8 combine.1
Async XLA Ops:
  2.3 47.6 %all-to-all-start = ((bf16[64,4,896]{2,1,0:T(4,128)(2,1)}), bf16[64,4,896]{2,1,0:T(4,128)(2,1)S(1)}, u32[]{:S(2)}, u32[]{:S(2)}) async-start(bf16[64,4,896]{2,1,0:T(4,128)(2,1)} %get-tuple-element.15), calls=%async_computation | async-start | bytes 917504 | tf_op jit(solution)/shard_map/all_to_all | solution.py:281
  21.1 35.1 %collective-permute-start.2 = (bf16[192,1792]{1,0:T(8,128)(2,1)}, bf16[192,1792]{1,0:T(8,128)(2,1)S(1)}, u32[]{:S(2)}, u32[]{:S(2)}) collective-permute-start(bf16[192,1792]{1,0:T(8,128)(2,1)} %get-tuple-element.17), channel_id=1, source_target_pairs={{0,4},{1,5},{2,6},{3,7},{4,0},{5,1},{6,2},{7,3},{8,12},{9,13},{10,... | collective-permute-start | bytes 2064392 | tf_op jit(solution)/shard_map/ppermute | solution.py:278
  28.6 27.7 %collective-permute-start.1 = (bf16[192,1792]{1,0:T(8,128)(2,1)}, bf16[192,1792]{1,0:T(8,128)(2,1)S(1)}, u32[]{:S(2)}, u32[]{:S(2)}) collective-permute-start(bf16[192,1792]{1,0:T(8,128)(2,1)} %get-tuple-element.16), channel_id=1, source_target_pairs={{0,2},{1,3},{2,4},{3,5},{4,6},{5,7},{6,0},{7,1},{8,10},{9,11},{10,... | collective-permute-start | bytes 2064392 | tf_op jit(solution)/shard_map/ppermute | solution.py:278
  31.2 25.3 %collective-permute-start.3 = (bf16[192,1792]{1,0:T(8,128)(2,1)}, bf16[192,1792]{1,0:T(8,128)(2,1)S(1)}, u32[]{:S(2)}, u32[]{:S(2)}) collective-permute-start(bf16[192,1792]{1,0:T(8,128)(2,1)} %get-tuple-element.18), channel_id=1, source_target_pairs={{0,6},{1,7},{2,0},{3,1},{4,2},{5,3},{6,4},{7,5},{8,14},{9,15},{10,... | collective-permute-start | bytes 2064392 | tf_op jit(solution)/shard_map/ppermute | solution.py:278
  50.8 11.5 %collective-permute-start = (bf16[256,896]{1,0:T(8,128)(2,1)}, bf16[256,896]{1,0:T(8,128)(2,1)S(1)}, u32[]{:S(2)}, u32[]{:S(2)}) collective-permute-start(bf16[256,896]{1,0:T(8,128)(2,1)} %reshape.6.rows_ref), channel_id=1, source_target_pairs={{0,1},{1,0},{2,3},{3,2},{4,5},{5,4},{6,7},{7,6},{8,9},{9,8},{10,11... | collective-permute-start | bytes 1376264 | tf_op jit(solution)/shard_map/ppermute | solution.py:285
  56.2 4.3 %copy-start = (bf16[128,1792]{1,0:T(8,128)(2,1)S(1)}, bf16[128,1792]{1,0:T(8,128)(2,1)}, u32[]{:S(2)}) copy-start(bf16[128,1792]{1,0:T(8,128)(2,1)} %cut.3.refs_0_) | copy-start | bytes 1376260
  56.4 0.9 copy-start.1
  58.2 21.0 %collective-permute-start.4 = (bf16[256,896]{1,0:T(8,128)(2,1)}, bf16[256,896]{1,0:T(8,128)(2,1)S(1)}, u32[]{:S(2)}, u32[]{:S(2)}) collective-permute-start(bf16[256,896]{1,0:T(8,128)(2,1)} %get-tuple-element.22), channel_id=1, source_target_pairs={{0,1},{1,0},{2,3},{3,2},{4,5},{5,4},{6,7},{7,6},{8,9},{9,8},{10,11... | collective-permute-start | bytes 1376264 | tf_op jit(solution)/shard_map/ppermute | solution.py:214
  63.7 4.5 %copy-start.2 = (s32[16,8]{0,1:T(8,128)S(1)}, s32[16,8]{0,1:T(8,128)}, u32[]{:S(2)}) copy-start(s32[16,8]{0,1:T(8,128)} %param.7) | copy-start | bytes 1540
  63.7 4.5 %copy-start.3 = (f32[16,8]{0,1:T(8,128)S(1)}, f32[16,8]{0,1:T(8,128)}, u32[]{:S(2)}) copy-start(f32[16,8]{0,1:T(8,128)} %param.8) | copy-start | bytes 1540
  63.7 11.3 %all-to-all-start.1 = ((bf16[4,128,256]{2,1,0:T(8,128)(2,1)}), bf16[4,128,256]{2,1,0:T(8,128)(2,1)S(1)}, u32[]{:S(2)}, u32[]{:S(2)}) async-start(bf16[4,128,256]{2,1,0:T(8,128)(2,1)} %far.1), calls=%async_computation.1 | async-start | bytes 524288 | tf_op jit(solution)/shard_map/all_to_all | solution.py:305
  75.8 10.8 %all-to-all-start.2 = ((bf16[8,64,256]{2,1,0:T(8,128)(2,1)}), bf16[8,64,256]{2,1,0:T(8,128)(2,1)S(1)}, u32[]{:S(2)}, u32[]{:S(2)}) async-start(bf16[8,64,256]{2,1,0:T(8,128)(2,1)} %hidden.1), calls=%async_computation.2 | async-start | bytes 524288 | tf_op jit(solution)/shard_map/all_to_all | solution.py:315
  87.1 8.9 %collective-permute-start.5 = (bf16[32,4,896]{2,1,0:T(4,128)(2,1)S(1)}, bf16[32,4,896]{2,1,0:T(4,128)(2,1)S(1)}, u32[]{:S(2)}, u32[]{:S(2)}) collective-permute-start(bf16[32,4,896]{2,1,0:T(4,128)(2,1)S(1)} %get-tuple-element.24), channel_id=1, source_target_pairs={{0,8},{8,0},{16,24},{24,16},{32,40},{40,32},{48,56},{56,48},{64,72... | collective-permute-start | bytes 688136 | tf_op jit(solution)/shard_map/ppermute | solution.py:324

commit v3 on v2

--- a/solution.py
+++ b/solution.py
@@ -224,12 +224,10 @@
     dims = (((0,), (0,)), ((), ()))
     total = lax.dot_general(held[0], near_ref[...], dims, preferred_element_type=F32)
     total = total + lax.dot_general(held[1], far_ref[...], dims, preferred_element_type=F32)
-    peers, slots, width = keep_ref.shape
-    half = lax.rem(lax.axis_index("expert"), 2)
-    rows = total.astype(BF16).reshape(peers, 2, slots, width)
-    even, odd = rows[:, 0], rows[:, 1]
-    keep_ref[...] = jnp.where(half == 0, even, odd)
-    give_ref[...] = jnp.where(half == 0, odd, even)
+    rows = total.astype(BF16)
+    kept = rows.shape[0] // 2
+    keep_ref[...] = rows[:kept].reshape(keep_ref.shape)
+    give_ref[...] = rows[kept:].reshape(give_ref.shape)
 
 
 def body(tokens, expert_ids, route_weights, gate_weight, up_weight, down_weight):
@@ -248,14 +246,14 @@
     part = jax.ShapeDtypeStruct((3 * units, wide), BF16)
     whole = pl.BlockSpec(memory_space=pl.ANY)
     packed, across = pl.pallas_call(
-        lambda *refs: pack_kernel(2, 2, *refs),
-        out_shape=[jax.ShapeDtypeStruct((devices_wide, capacity, width), BF16), part],
+        lambda *refs: pack_kernel(1, 2, *refs),
+        out_shape=[jax.ShapeDtypeStruct((experts, capacity, width), BF16), part],
         in_specs=[whole] * 5,
         out_specs=[whole] * 2,
         scratch_shapes=[
             pltpu.VMEM(ids.shape, jnp.int32),
             pltpu.VMEM(tokens.shape, BF16),
-            pltpu.VMEM((devices_wide, capacity, width), BF16),
+            pltpu.VMEM((experts, capacity, width), BF16),
             pltpu.VMEM(part.shape, BF16),
             pltpu.SemaphoreType.DMA((3,)),
             pltpu.SemaphoreType.DMA((2,)),
@@ -270,17 +268,27 @@
         name="mix",
     )(ids, route_weights.T)
 
-    ahead, behind = cut((1, 3), weights, wide)
+    ahead, behind = cut((1, 3), weights[:2], wide)
     (own,) = cut((0,), weights[:2], wide)
-    (own_down,) = cut((0,), weights[2:], wide)
+    down_ahead, down_behind, own_down = cut((1, 3, 0), weights[2:], wide)
     blocks = [own, ahead, across, behind]
     for ring in range(1, rings):
         blocks[ring] = lax.ppermute(
             blocks[ring], "tensor", shift_pairs(groups, ring, 0)
         )
-    arrived = lax.all_to_all(packed, "expert", 0, 0, tiled=True)
-    arrived = arrived.reshape(arrived_count, width)
-    down_near, down_far = down_columns([own_down, *blocks[1:]], width, groups)
+    down_ahead = lax.ppermute(down_ahead, "tensor", shift_pairs(groups, 1, 0))
+    down_behind = lax.ppermute(down_behind, "tensor", shift_pairs(groups, 3, 0))
+    same_half = [list(range(half, devices_wide, 2)) for half in range(2)]
+    pairs = [(i, i + 1 - 2 * (i % 2)) for i in range(devices_wide)]
+    arrived = lax.all_to_all(
+        packed, "expert", 0, 0, axis_index_groups=same_half, tiled=True
+    )
+    arrived = arrived.reshape(experts * capacity, width)
+    theirs = lax.ppermute(arrived, "expert", pairs)
+    arrived = jnp.concatenate([arrived, theirs], axis=0)
+    down_near, down_far = down_columns(
+        [own_down, down_ahead, blocks[2], down_behind], width, groups
+    )
 
     partner = lax.ppermute(arrived, "tensor", shift_pairs(groups, 0, 1))
     near = pl.pallas_call(
@@ -320,10 +328,8 @@
         compiler_params=pltpu.CompilerParams(vmem_limit_bytes=VMEM_BYTES),
         name="down",
     )(hidden, down_near, down_far)
-    pairs = [(i, i + 1 - 2 * (i % 2)) for i in range(devices_wide)]
     taken = lax.ppermute(given, "expert", pairs)
     both = (kept.astype(F32) + taken.astype(F32)).astype(BF16)
-    same_half = [list(range(half, devices_wide, 2)) for half in range(2)]
     returned = lax.all_to_all(
         both, "expert", 0, 0, axis_index_groups=same_half, tiled=True
     )

time: 130 us -> 152 us (1.17)
  blocking collectives: 30.9 us -> 62 us
  starting transfers between devices: 46.2 us -> 34.1 us
  waiting for transfers between devices: 34.2 us -> 37.7 us
    all_to_all x0 -> x1, blocking collectives: none -> 35.8 us  [body(): lax.all_to_all(packed, 'expert', 0, 0, axis_index_groups=same_half, tiled...]
    all_to_all x1 -> x0, starting transfers between devices: 18.8 us -> none  [body(): arrived = lax.all_to_all(packed, 'expert', 0, 0, tiled=True)]
    ppermute x0 -> x3, waiting for transfers between devices: none -> 16.5 us  [the longest x1 11.5 us: body(): down_ahead = lax.ppermute(down_ahead, 'tensor', shift_pairs(groups, 1, 0))]
    all_to_all x1 -> x0, waiting for transfers between devices: 14.2 us -> none  [body(): arrived = lax.all_to_all(packed, 'expert', 0, 0, tiled=True)]
    ppermute x0 -> x3, starting transfers between devices: none -> 8.02 us  [the longest x1 3.46 us: body(): theirs = lax.ppermute(arrived, 'expert', pairs)]
    all_to_all x1, blocking collectives: 30.9 us -> 26.2 us  [body(): lax.all_to_all(both, 'expert', 0, 0, axis_index_groups=same_half, tiled=T...]
  transfers between devices with their start and end apart: 9 -> 11, of which waited for: 5 -> 5; matrix products, arithmetic and copies ran while one was open for 1% -> 1% of each run, Pallas kernels for 8% -> 7%
where the time goes in v3:
time: 152 us; the launch traced here: 150 us
  blocking collectives  62 us (41%)
  waiting for transfers between devices  37.7 us (25%)
  starting transfers between devices  34.1 us (22%)
  Pallas kernels  14.4 us (9%)
  local copies, waits for them, and re-layouts  1.57 us (1%)
    all_to_all x1, blocking collectives, body(): lax.all_to_all(packed, 'expert', 0, 0, axis_index_groups=same_half, tiled...  35.8 us
    all_to_all x1, blocking collectives, body(): lax.all_to_all(both, 'expert', 0, 0, axis_index_groups=same_half, tiled=T...  26.2 us
    ppermute x3, starting transfers between devices, body(): lax.ppermute(blocks[ring], 'tensor', shift_pairs(groups, ring, 0))  12.2 us
    ppermute x1, waiting for transfers between devices, body(): down_ahead = lax.ppermute(down_ahead, 'tensor', shift_pairs(groups, 1, 0))  11.5 us
    all_to_all x1, waiting for transfers between devices, body(): hidden = lax.all_to_all(hidden, 'tensor', 0, 0, tiled=True)  7.42 us
    all_to_all x1, waiting for transfers between devices, body(): lax.all_to_all(partial, 'tensor', 0, 0, axis_index_groups=same_core, tile...  7.13 us
    ppermute x1, waiting for transfers between devices, body(): taken = lax.ppermute(given, 'expert', pairs)  6.66 us
    pallas_call x3, Pallas kernels, cut(): pl.pallas_call(lambda *refs: cut_kernel(rings, *refs), out_shape=[shape]...  5.92 us
  transfers between devices with their start and end apart: 11, of which 5 were waited for; matrix products, arithmetic and copies ran while one was open for 1% of the time, Pallas kernels for 7%

profile of v3, /device:TPU:6, one launch (start us, length us, event | category | flops | bytes accessed | tf_op | source)
XLA Modules:
  0.0 150.1 jit_solution(8571708009004628698)
XLA Ops:
  0.0 2.2 %pack.1 = (bf16[32,4,896]{2,1,0:T(4,128)(2,1)}, bf16[192,1792]{1,0:T(8,128)(2,1)}) custom-call(s32[8,16]{1,0:T(8,128)} %bitcast.5, bf16[16,896]{1,0:T(8,128)(2,1)} %refs_1_.1, bf16[64,7168]{1,0:T(8,128)(2,1)} %bitcast.8, bf16[64,7168]{1,0:T(8,128)(2,1)} %bitcast.11, bf16[64,7168]{1,0:T(8,128)(2,1)} %bitcast.14), custom_call_target="tpu_custom_call" | custom-call | tf_op jit(solution)/shard_map/pack/pallas_call | solution.py:248
  2.2 35.8 %all_to_all.20 = bf16[32,4,896]{2,1,0:T(4,128)(2,1)S(1)} all-to-all(bf16[32,4,896]{2,1,0:T(4,128)(2,1)} %get-tuple-element.18), channel_id=1, replica_groups={{0,16,32,48,64,80,96,112,128,144,160,176,192,208,224,240,256,272,288,30..., dimensions={0} | all-to-all | bytes 458752 | tf_op jit(solution)/shard_map/all_to_all | solution.py:283
  38.0 0.1 reshape.6
  38.1 3.5 %collective-permute-start = (bf16[128,896]{1,0:T(8,128)(2,1)S(1)}, bf16[128,896]{1,0:T(8,128)(2,1)S(1)}, u32[]{:S(2)}, u32[]{:S(2)}) collective-permute-start(bf16[128,896]{1,0:T(8,128)(2,1)S(1)} %reshape.6), channel_id=1, source_target_pairs={{0,8},{8,0},{16,24},{24,16},{32,40},{40,32},{48,56},{56,48},{64,72... | collective-permute-start | bytes 688136 | tf_op jit(solution)/shard_map/ppermute | solution.py:287
  41.5 5.1 %collective-permute-start.3 = (bf16[192,1792]{1,0:T(8,128)(2,1)}, bf16[192,1792]{1,0:T(8,128)(2,1)S(1)}, u32[]{:S(2)}, u32[]{:S(2)}) collective-permute-start(bf16[192,1792]{1,0:T(8,128)(2,1)} %get-tuple-element.20), channel_id=1, source_target_pairs={{0,4},{1,5},{2,6},{3,7},{4,0},{5,1},{6,2},{7,3},{8,12},{9,13},{10,... | collective-permute-start | bytes 2064392 | tf_op jit(solution)/shard_map/ppermute | solution.py:276
  46.6 2.1 %cut.4 = (bf16[128,1792]{1,0:T(8,128)(2,1)}, bf16[128,1792]{1,0:T(8,128)(2,1)}) custom-call(bf16[64,7168]{1,0:T(8,128)(2,1)} %bitcast.9, bf16[64,7168]{1,0:T(8,128)(2,1)} %bitcast.12), custom_call_target="tpu_custom_call" | custom-call | tf_op jit(solution)/shard_map/cut/pallas_call | solution.py:132
  48.8 2.6 %collective-permute-start.2 = (bf16[128,1792]{1,0:T(8,128)(2,1)}, bf16[128,1792]{1,0:T(8,128)(2,1)S(1)}, u32[]{:S(2)}, u32[]{:S(2)}) collective-permute-start(bf16[128,1792]{1,0:T(8,128)(2,1)} %get-tuple-element.19), channel_id=1, source_target_pairs={{0,2},{1,3},{2,4},{3,5},{4,6},{5,7},{6,0},{7,1},{8,10},{9,11},{10,... | collective-permute-start | bytes 1376264 | tf_op jit(solution)/shard_map/ppermute | solution.py:276
  51.4 4.5 %collective-permute-start.4 = (bf16[128,1792]{1,0:T(8,128)(2,1)}, bf16[128,1792]{1,0:T(8,128)(2,1)S(1)}, u32[]{:S(2)}, u32[]{:S(2)}) collective-permute-start(bf16[128,1792]{1,0:T(8,128)(2,1)} %get-tuple-element.21), channel_id=1, source_target_pairs={{0,6},{1,7},{2,0},{3,1},{4,2},{5,3},{6,4},{7,5},{8,14},{9,15},{10,... | collective-permute-start | bytes 1376264 | tf_op jit(solution)/shard_map/ppermute | solution.py:276
  55.8 1.9 %cut.5 = (bf16[64,1792]{1,0:T(8,128)(2,1)}, bf16[64,1792]{1,0:T(8,128)(2,1)}, bf16[64,1792]{1,0:T(8,128)(2,1)}) custom-call(bf16[64,7168]{1,0:T(8,128)(2,1)} %bitcast.15), custom_call_target="tpu_custom_call" | custom-call | tf_op jit(solution)/shard_map/cut/pallas_call | solution.py:132
  57.8 1.9 %collective-permute-start.5 = (bf16[64,1792]{1,0:T(8,128)(2,1)}, bf16[64,1792]{1,0:T(8,128)(2,1)S(1)}, u32[]{:S(2)}, u32[]{:S(2)}) collective-permute-start(bf16[64,1792]{1,0:T(8,128)(2,1)} %get-tuple-element.25), channel_id=1, source_target_pairs={{0,2},{1,3},{2,4},{3,5},{4,6},{5,7},{6,0},{7,1},{8,10},{9,11},{10,... | collective-permute-start | bytes 688136 | tf_op jit(solution)/shard_map/ppermute | solution.py:279
  59.7 0.7 constant_dynamic-update-slice_fusion.1
  60.4 0.0 copy-start.4
  60.4 0.0 collective-permute-done
  60.4 0.7 constant_dynamic-update-slice_fusion.rows_ref
  61.1 1.9 %collective-permute-start.1 = (bf16[256,896]{1,0:T(8,128)(2,1)}, bf16[256,896]{1,0:T(8,128)(2,1)S(1)}, u32[]{:S(2)}, u32[]{:S(2)}) collective-permute-start(bf16[256,896]{1,0:T(8,128)(2,1)} %constant_dynamic-update-slice_fusion.rows_ref), channel_id=1, source_target_pairs={{0,1},{1,0},{2,3},{3,2},{4,5},{5,4},{6,7},{7,6},{8,9},{9,8},{10,11... | collective-permute-start | bytes 1376264 | tf_op jit(solution)/shard_map/ppermute | solution.py:293
  63.0 11.5 %collective-permute-done.5.refs_1_ = bf16[64,1792]{1,0:T(8,128)(2,1)S(1)} collective-permute-done((bf16[64,1792]{1,0:T(8,128)(2,1)}, bf16[64,1792]{1,0:T(8,128)(2,1)S(1)}, u32[]{:S(2)}, u32[]{:S(2)}) %collective-permute-start.5) | collective-permute-done | bytes 229408 | tf_op jit(solution)/shard_map/ppermute | solution.py:279
  74.5 0.0 copy-done.4
  74.5 2.6 %collective-permute-start.6 = (bf16[64,1792]{1,0:T(8,128)(2,1)S(1)}, bf16[64,1792]{1,0:T(8,128)(2,1)S(1)}, u32[]{:S(2)}, u32[]{:S(2)}) collective-permute-start(bf16[64,1792]{1,0:T(8,128)(2,1)S(1)} %copy-done.4), channel_id=1, source_target_pairs={{0,6},{1,7},{2,0},{3,1},{4,2},{5,3},{6,4},{7,5},{8,14},{9,15},{10,... | collective-permute-start | bytes 688136 | tf_op jit(solution)/shard_map/ppermute | solution.py:280
  77.2 1.9 %cut.3.refs_0_ = bf16[128,1792]{1,0:T(8,128)(2,1)} custom-call(bf16[64,7168]{1,0:T(8,128)(2,1)} %bitcast.10, bf16[64,7168]{1,0:T(8,128)(2,1)} %bitcast.13), custom_call_target="tpu_custom_call" | custom-call | tf_op jit(solution)/shard_map/cut/pallas_call | solution.py:132
  79.1 5.0 %collective-permute-done.6.refs_3_ = bf16[64,1792]{1,0:T(8,128)(2,1)S(1)} collective-permute-done((bf16[64,1792]{1,0:T(8,128)(2,1)S(1)}, bf16[64,1792]{1,0:T(8,128)(2,1)S(1)}, u32[]{:S(2)}, u32[]{:S(2)}) %collective-permute-start.6) | collective-permute-done | bytes 229408 | tf_op jit(solution)/shard_map/ppermute | solution.py:280
  84.1 0.0 collective-permute-done.3.refs_2_
  84.1 0.0 copy-done.1
  84.1 0.9 core_cut.1
  85.0 1.9 %collective-permute-start.7 = (bf16[256,896]{1,0:T(8,128)(2,1)}, bf16[256,896]{1,0:T(8,128)(2,1)S(1)}, u32[]{:S(2)}, u32[]{:S(2)}) collective-permute-start(bf16[256,896]{1,0:T(8,128)(2,1)} %get-tuple-element.28), channel_id=1, source_target_pairs={{0,1},{1,0},{2,3},{3,2},{4,5},{5,4},{6,7},{7,6},{8,9},{9,8},{10,11... | collective-permute-start | bytes 1376264 | tf_op jit(solution)/shard_map/ppermute | solution.py:214
  86.9 0.0 collective-permute-done.2.refs_1_
  86.9 0.0 collective-permute-done.4.refs_3_
  86.9 0.0 copy-done
  86.9 1.7 %near.1.near_ref = f32[4,128,256]{2,1,0:T(8,128)S(1)} custom-call(bf16[256,896]{1,0:T(8,128)(2,1)} %constant_dynamic-update-slice_fusion.rows_ref, bf16[128,1792]{1,0:T(8,128)(2,1)S(1)} %copy-done, bf16[128,1792]{1,0:T(8,128)(2,1)S(1)} %collective-permute-done.2.refs_1_, bf16[192,1792]{1,0:T(8,128)(2,1)S(1)} %collective-permute-done.3.refs_2_, ...), custom_call_target="tpu_custom_call" | custom-call | flops 1000000000 | bytes 1000000 | tf_op jit(solution)/shard_map/near/pallas_call | solution.py:294
  88.6 0.0 collective-permute-done.1.rows_ref
  88.7 1.4 far.1
  90.1 0.0 copy-start.2
  90.1 0.0 copy-start.3
  90.1 4.5 %all-to-all-start.1 = ((bf16[4,128,256]{2,1,0:T(8,128)(2,1)}), bf16[4,128,256]{2,1,0:T(8,128)(2,1)S(1)}, u32[]{:S(2)}, u32[]{:S(2)}) async-start(bf16[4,128,256]{2,1,0:T(8,128)(2,1)} %far.1), calls=%async_computation.1 | async-start | bytes 524288 | tf_op jit(solution)/shard_map/all_to_all | solution.py:313
  94.6 0.0 copy-done.2
  94.6 0.0 copy-done.3
  94.6 0.2 mix.1.mix_ref
  94.8 7.1 %all-to-all-done.1.partial_ref = bf16[4,128,256]{2,1,0:T(8,128)(2,1)S(1)} async-done(((bf16[4,128,256]{2,1,0:T(8,128)(2,1)}), bf16[4,128,256]{2,1,0:T(8,128)(2,1)S(1)}, u32[]{:S(2)}, u32[]{:S(2)}) %all-to-all-start.1) | async-done | bytes 262176 | tf_op jit(solution)/shard_map/all_to_all | solution.py:313
  101.9 0.7 hidden.1
  102.7 3.4 %all-to-all-start.2 = ((bf16[8,64,256]{2,1,0:T(8,128)(2,1)}), bf16[8,64,256]{2,1,0:T(8,128)(2,1)S(1)}, u32[]{:S(2)}, u32[]{:S(2)}) async-start(bf16[8,64,256]{2,1,0:T(8,128)(2,1)} %hidden.1), calls=%async_computation.2 | async-start | bytes 524288 | tf_op jit(solution)/shard_map/all_to_all | solution.py:323
  106.1 0.0 collective-permute-done.7.far_ref
  106.1 7.4 %all-to-all-done.2.hidden_ref = bf16[8,64,256]{2,1,0:T(8,128)(2,1)S(1)} async-done(((bf16[8,64,256]{2,1,0:T(8,128)(2,1)}), bf16[8,64,256]{2,1,0:T(8,128)(2,1)S(1)}, u32[]{:S(2)}, u32[]{:S(2)}) %all-to-all-start.2) | async-done | bytes 262176 | tf_op jit(solution)/shard_map/all_to_all | solution.py:323
  113.5 0.5 down.1
  114.0 2.2 %collective-permute-start.8 = (bf16[32,4,896]{2,1,0:T(4,128)(2,1)S(1)}, bf16[32,4,896]{2,1,0:T(4,128)(2,1)S(1)}, u32[]{:S(2)}, u32[]{:S(2)}) collective-permute-start(bf16[32,4,896]{2,1,0:T(4,128)(2,1)S(1)} %get-tuple-element.30), channel_id=1, source_target_pairs={{0,8},{8,0},{16,24},{24,16},{32,40},{40,32},{48,56},{56,48},{64,72... | collective-permute-start | bytes 688136 | tf_op jit(solution)/shard_map/ppermute | solution.py:331
  116.2 6.7 %collective-permute-done.8 = bf16[32,4,896]{2,1,0:T(4,128)(2,1)S(1)} collective-permute-done((bf16[32,4,896]{2,1,0:T(4,128)(2,1)S(1)}, bf16[32,4,896]{2,1,0:T(4,128)(2,1)S(1)}, u32[]{:S(2)}, u32[]{:S(2)}) %collective-permute-start.8) | collective-permute-done | bytes 229408 | tf_op jit(solution)/shard_map/ppermute | solution.py:331
  122.9 0.1 add_convert_fusion
  123.0 26.2 %all_to_all.21 = bf16[32,4,896]{2,1,0:T(4,128)(2,1)S(1)} all-to-all(bf16[32,4,896]{2,1,0:T(4,128)(2,1)S(1)} %add_convert_fusion), channel_id=1, replica_groups={{0,16,32,48,64,80,96,112,128,144,160,176,192,208,224,240,256,272,288,30..., dimensions={0} | all-to-all | bytes 458752 | tf_op jit(solution)/shard_map/all_to_all | solution.py:333
  149.2 0.1 reshape.7.rows_ref
  149.3 0.8 combine.1
  (2 shorter events, 0.0 us)
Async XLA Ops:
  38.1 22.3 %collective-permute-start = (bf16[128,896]{1,0:T(8,128)(2,1)S(1)}, bf16[128,896]{1,0:T(8,128)(2,1)S(1)}, u32[]{:S(2)}, u32[]{:S(2)}) collective-permute-start(bf16[128,896]{1,0:T(8,128)(2,1)S(1)} %reshape.6), channel_id=1, source_target_pairs={{0,8},{8,0},{16,24},{24,16},{32,40},{40,32},{48,56},{56,48},{64,72... | collective-permute-start | bytes 688136 | tf_op jit(solution)/shard_map/ppermute | solution.py:287
  41.5 42.6 %collective-permute-start.3 = (bf16[192,1792]{1,0:T(8,128)(2,1)}, bf16[192,1792]{1,0:T(8,128)(2,1)S(1)}, u32[]{:S(2)}, u32[]{:S(2)}) collective-permute-start(bf16[192,1792]{1,0:T(8,128)(2,1)} %get-tuple-element.20), channel_id=1, source_target_pairs={{0,4},{1,5},{2,6},{3,7},{4,0},{5,1},{6,2},{7,3},{8,12},{9,13},{10,... | collective-permute-start | bytes 2064392 | tf_op jit(solution)/shard_map/ppermute | solution.py:276
  48.8 38.1 %collective-permute-start.2 = (bf16[128,1792]{1,0:T(8,128)(2,1)}, bf16[128,1792]{1,0:T(8,128)(2,1)S(1)}, u32[]{:S(2)}, u32[]{:S(2)}) collective-permute-start(bf16[128,1792]{1,0:T(8,128)(2,1)} %get-tuple-element.19), channel_id=1, source_target_pairs={{0,2},{1,3},{2,4},{3,5},{4,6},{5,7},{6,0},{7,1},{8,10},{9,11},{10,... | collective-permute-start | bytes 1376264 | tf_op jit(solution)/shard_map/ppermute | solution.py:276
  51.4 35.5 %collective-permute-start.4 = (bf16[128,1792]{1,0:T(8,128)(2,1)}, bf16[128,1792]{1,0:T(8,128)(2,1)S(1)}, u32[]{:S(2)}, u32[]{:S(2)}) collective-permute-start(bf16[128,1792]{1,0:T(8,128)(2,1)} %get-tuple-element.21), channel_id=1, source_target_pairs={{0,6},{1,7},{2,0},{3,1},{4,2},{5,3},{6,4},{7,5},{8,14},{9,15},{10,... | collective-permute-start | bytes 1376264 | tf_op jit(solution)/shard_map/ppermute | solution.py:276
  57.8 16.8 %collective-permute-start.5 = (bf16[64,1792]{1,0:T(8,128)(2,1)}, bf16[64,1792]{1,0:T(8,128)(2,1)S(1)}, u32[]{:S(2)}, u32[]{:S(2)}) collective-permute-start(bf16[64,1792]{1,0:T(8,128)(2,1)} %get-tuple-element.25), channel_id=1, source_target_pairs={{0,2},{1,3},{2,4},{3,5},{4,6},{5,7},{6,0},{7,1},{8,10},{9,11},{10,... | collective-permute-start | bytes 688136 | tf_op jit(solution)/shard_map/ppermute | solution.py:279
  60.4 14.2 %copy-start.4 = (bf16[64,1792]{1,0:T(8,128)(2,1)S(1)}, bf16[64,1792]{1,0:T(8,128)(2,1)}, u32[]{:S(2)}) copy-start(bf16[64,1792]{1,0:T(8,128)(2,1)} %get-tuple-element.26) | copy-start | bytes 688132
  61.1 27.5 %collective-permute-start.1 = (bf16[256,896]{1,0:T(8,128)(2,1)}, bf16[256,896]{1,0:T(8,128)(2,1)S(1)}, u32[]{:S(2)}, u32[]{:S(2)}) collective-permute-start(bf16[256,896]{1,0:T(8,128)(2,1)} %constant_dynamic-update-slice_fusion.rows_ref), channel_id=1, source_target_pairs={{0,1},{1,0},{2,3},{3,2},{4,5},{5,4},{6,7},{7,6},{8,9},{9,8},{10,11... | collective-permute-start | bytes 1376264 | tf_op jit(solution)/shard_map/ppermute | solution.py:293
  74.5 9.5 %copy-start.1 = (bf16[64,1792]{1,0:T(8,128)(2,1)S(1)}, bf16[64,1792]{1,0:T(8,128)(2,1)}, u32[]{:S(2)}) copy-start(bf16[64,1792]{1,0:T(8,128)(2,1)} %get-tuple-element.24.refs_0_) | copy-start | bytes 688132
  74.5 9.5 %collective-permute-start.6 = (bf16[64,1792]{1,0:T(8,128)(2,1)S(1)}, bf16[64,1792]{1,0:T(8,128)(2,1)S(1)}, u32[]{:S(2)}, u32[]{:S(2)}) collective-permute-start(bf16[64,1792]{1,0:T(8,128)(2,1)S(1)} %copy-done.4), channel_id=1, source_target_pairs={{0,6},{1,7},{2,0},{3,1},{4,2},{5,3},{6,4},{7,5},{8,14},{9,15},{10,... | collective-permute-start | bytes 688136 | tf_op jit(solution)/shard_map/ppermute | solution.py:280
  84.1 2.8 %copy-start = (bf16[128,1792]{1,0:T(8,128)(2,1)S(1)}, bf16[128,1792]{1,0:T(8,128)(2,1)}, u32[]{:S(2)}) copy-start(bf16[128,1792]{1,0:T(8,128)(2,1)} %cut.3.refs_0_) | copy-start | bytes 1376260
  85.0 21.1 %collective-permute-start.7 = (bf16[256,896]{1,0:T(8,128)(2,1)}, bf16[256,896]{1,0:T(8,128)(2,1)S(1)}, u32[]{:S(2)}, u32[]{:S(2)}) collective-permute-start(bf16[256,896]{1,0:T(8,128)(2,1)} %get-tuple-element.28), channel_id=1, source_target_pairs={{0,1},{1,0},{2,3},{3,2},{4,5},{5,4},{6,7},{7,6},{8,9},{9,8},{10,11... | collective-permute-start | bytes 1376264 | tf_op jit(solution)/shard_map/ppermute | solution.py:214
  90.1 4.5 %copy-start.2 = (s32[16,8]{0,1:T(8,128)S(1)}, s32[16,8]{0,1:T(8,128)}, u32[]{:S(2)}) copy-start(s32[16,8]{0,1:T(8,128)} %param.7) | copy-start | bytes 1540
  90.1 4.5 %copy-start.3 = (f32[16,8]{0,1:T(8,128)S(1)}, f32[16,8]{0,1:T(8,128)}, u32[]{:S(2)}) copy-start(f32[16,8]{0,1:T(8,128)} %param.8) | copy-start | bytes 1540
  90.1 11.8 %all-to-all-start.1 = ((bf16[4,128,256]{2,1,0:T(8,128)(2,1)}), bf16[4,128,256]{2,1,0:T(8,128)(2,1)S(1)}, u32[]{:S(2)}, u32[]{:S(2)}) async-start(bf16[4,128,256]{2,1,0:T(8,128)(2,1)} %far.1), calls=%async_computation.1 | async-start | bytes 524288 | tf_op jit(solution)/shard_map/all_to_all | solution.py:313
  102.7 10.8 %all-to-all-start.2 = ((bf16[8,64,256]{2,1,0:T(8,128)(2,1)}), bf16[8,64,256]{2,1,0:T(8,128)(2,1)S(1)}, u32[]{:S(2)}, u32[]{:S(2)}) async-start(bf16[8,64,256]{2,1,0:T(8,128)(2,1)} %hidden.1), calls=%async_computation.2 | async-start | bytes 524288 | tf_op jit(solution)/shard_map/all_to_all | solution.py:323
  114.0 8.9 %collective-permute-start.8 = (bf16[32,4,896]{2,1,0:T(4,128)(2,1)S(1)}, bf16[32,4,896]{2,1,0:T(4,128)(2,1)S(1)}, u32[]{:S(2)}, u32[]{:S(2)}) collective-permute-start(bf16[32,4,896]{2,1,0:T(4,128)(2,1)S(1)} %get-tuple-element.30), channel_id=1, source_target_pairs={{0,8},{8,0},{16,24},{24,16},{32,40},{40,32},{48,56},{56,48},{64,72... | collective-permute-start | bytes 688136 | tf_op jit(solution)/shard_map/ppermute | solution.py:331

commit v4 on v2

--- a/solution.py
+++ b/solution.py
@@ -40,7 +40,7 @@
         fetch.wait()
     select, _ = slot_onehot(ids[...], peers * capacity, capacity, copies)
     rows = jnp.dot(select.astype(BF16), tok[...], preferred_element_type=F32)
-    packed[...] = rows.reshape(peers, capacity, width).astype(BF16)
+    packed[...] = rows.astype(BF16).reshape(peers, capacity, width)
     for read in reads:
         read.wait()
     writes = [
@@ -214,22 +214,19 @@
     return near, lax.ppermute(far, "tensor", shift_pairs(groups, 0, 1))
 
 
-def down_kernel(hidden_ref, near_ref, far_ref, keep_ref, give_ref, held):
-    groups, units, _ = hidden_ref.shape
+def down_kernel(other, hidden_ref, near_ref, far_ref, out_ref, held):
+    groups, units, count = hidden_ref.shape
     me = lax.axis_index("tensor")
+    parity = lax.rem(lax.axis_index("expert") + other, 2)
+    rows = pl.ds(pl.multiple_of(parity * (count // 2), 128), count // 2)
     for core in range(CORES):
         for ring in range(groups // CORES):
             source = moved_by(me, groups, ring, core, sign=-1)
-            held[core, pl.ds(ring * units, units), :] = hidden_ref[source]
+            held[core, pl.ds(ring * units, units), :] = hidden_ref[source, :, rows]
     dims = (((0,), (0,)), ((), ()))
     total = lax.dot_general(held[0], near_ref[...], dims, preferred_element_type=F32)
     total = total + lax.dot_general(held[1], far_ref[...], dims, preferred_element_type=F32)
-    peers, slots, width = keep_ref.shape
-    half = lax.rem(lax.axis_index("expert"), 2)
-    rows = total.astype(BF16).reshape(peers, 2, slots, width)
-    even, odd = rows[:, 0], rows[:, 1]
-    keep_ref[...] = jnp.where(half == 0, even, odd)
-    give_ref[...] = jnp.where(half == 0, odd, even)
+    out_ref[...] = total.astype(BF16).reshape(out_ref.shape)
 
 
 def body(tokens, expert_ids, route_weights, gate_weight, up_weight, down_weight):
@@ -279,7 +276,8 @@
             blocks[ring], "tensor", shift_pairs(groups, ring, 0)
         )
     arrived = lax.all_to_all(packed, "expert", 0, 0, tiled=True)
-    arrived = arrived.reshape(arrived_count, width)
+    arrived = arrived.reshape(experts, 2, capacity, width)
+    arrived = jnp.swapaxes(arrived, 0, 1).reshape(arrived_count, width)
     down_near, down_far = down_columns([own_down, *blocks[1:]], width, groups)
 
     partner = lax.ppermute(arrived, "tensor", shift_pairs(groups, 0, 1))
@@ -313,15 +311,22 @@
     )(partial)
     hidden, mix = lax.optimization_barrier((hidden, mix))
     hidden = lax.all_to_all(hidden, "tensor", 0, 0, tiled=True)
-    kept, given = pl.pallas_call(
-        down_kernel,
-        out_shape=[jax.ShapeDtypeStruct((experts, capacity, width), BF16)] * 2,
-        scratch_shapes=[pltpu.VMEM((2, groups // 2 * units, arrived_count), BF16)],
-        compiler_params=pltpu.CompilerParams(vmem_limit_bytes=VMEM_BYTES),
-        name="down",
-    )(hidden, down_near, down_far)
+
+    def product(other):
+        return pl.pallas_call(
+            lambda *refs: down_kernel(other, *refs),
+            out_shape=jax.ShapeDtypeStruct((experts, capacity, width), BF16),
+            scratch_shapes=[pltpu.VMEM((2, rings * units, arrived_count // 2), BF16)],
+            compiler_params=pltpu.CompilerParams(vmem_limit_bytes=VMEM_BYTES),
+            cost_estimate=pl.CostEstimate(
+                flops=10**8, bytes_accessed=10**6, transcendentals=0
+            ),
+            name="down",
+        )(hidden, down_near, down_far)
+
     pairs = [(i, i + 1 - 2 * (i % 2)) for i in range(devices_wide)]
-    taken = lax.ppermute(given, "expert", pairs)
+    taken = lax.ppermute(product(1), "expert", pairs)
+    kept = product(0)
     both = (kept.astype(F32) + taken.astype(F32)).astype(BF16)
     same_half = [list(range(half, devices_wide, 2)) for half in range(2)]
     returned = lax.all_to_all(
@@ -345,6 +350,7 @@
         P("expert", "tensor", None),
         P("expert", "tensor", None),
     )
+
     def step(*args):
         return body(*args)
 

time: 130 us -> 130 us (level)
  transfers between devices with their start and end apart: 9 -> 9, of which waited for: 5 -> 4; matrix products, arithmetic and copies ran while one was open for 1% -> 1% of each run, Pallas kernels for 8% -> 9%
where the time goes in v4:
time: 130 us; the launch traced here: 128 us
  starting transfers between devices  46.2 us (36%)
  waiting for transfers between devices  33.8 us (26%)
  blocking collectives  30.8 us (24%)
  Pallas kernels  14.7 us (11%)
  local copies, waits for them, and re-layouts  2.11 us (2%)
    all_to_all x1, blocking collectives, body(): lax.all_to_all(both, 'expert', 0, 0, axis_index_groups=same_half, tiled=T...  30.8 us
    all_to_all x1, starting transfers between devices, body(): arrived = lax.all_to_all(packed, 'expert', 0, 0, tiled=True)  18.8 us
    all_to_all x1, waiting for transfers between devices, body(): arrived = lax.all_to_all(packed, 'expert', 0, 0, tiled=True)  14.2 us
    ppermute x3, starting transfers between devices, body(): lax.ppermute(blocks[ring], 'tensor', shift_pairs(groups, ring, 0))  12.2 us
    all_to_all x1, waiting for transfers between devices, body(): hidden = lax.all_to_all(hidden, 'tensor', 0, 0, tiled=True)  7.42 us
    all_to_all x1, waiting for transfers between devices, body(): lax.all_to_all(partial, 'tensor', 0, 0, axis_index_groups=same_core, tile...  6.65 us
    pallas_call x3, Pallas kernels, cut(): pl.pallas_call(lambda *refs: cut_kernel(rings, *refs), out_shape=[shape]...  5.92 us
    ppermute x1, waiting for transfers between devices, body(): taken = lax.ppermute(product(1), 'expert', pairs)  5.49 us
  transfers between devices with their start and end apart: 9, of which 4 were waited for; matrix products, arithmetic and copies ran while one was open for 1% of the time, Pallas kernels for 9%

profile of v4, /device:TPU:6, one launch (start us, length us, event | category | flops | bytes accessed | tf_op | source)
XLA Modules:
  0.0 127.9 jit_solution(11866279135746166859)
XLA Ops:
  0.0 2.3 %pack.1 = (bf16[64,4,896]{2,1,0:T(4,128)(2,1)}, bf16[192,1792]{1,0:T(8,128)(2,1)}) custom-call(s32[8,16]{1,0:T(8,128)} %bitcast.9, bf16[16,896]{1,0:T(8,128)(2,1)} %refs_1_.1, bf16[64,7168]{1,0:T(8,128)(2,1)} %bitcast.12, bf16[64,7168]{1,0:T(8,128)(2,1)} %bitcast.15, bf16[64,7168]{1,0:T(8,128)(2,1)} %bitcast.18), custom_call_target="tpu_custom_call" | custom-call | tf_op jit(solution)/shard_map/pack/pallas_call | solution.py:247
  2.3 18.8 %all-to-all-start = ((bf16[64,4,896]{2,1,0:T(4,128)(2,1)}), bf16[64,4,896]{2,1,0:T(4,128)(2,1)S(1)}, u32[]{:S(2)}, u32[]{:S(2)}) async-start(bf16[64,4,896]{2,1,0:T(4,128)(2,1)} %get-tuple-element.13), calls=%async_computation | async-start | bytes 917504 | tf_op jit(solution)/shard_map/all_to_all | solution.py:278
  21.1 5.1 %collective-permute-start.2 = (bf16[192,1792]{1,0:T(8,128)(2,1)}, bf16[192,1792]{1,0:T(8,128)(2,1)S(1)}, u32[]{:S(2)}, u32[]{:S(2)}) collective-permute-start(bf16[192,1792]{1,0:T(8,128)(2,1)} %get-tuple-element.15), channel_id=1, source_target_pairs={{0,4},{1,5},{2,6},{3,7},{4,0},{5,1},{6,2},{7,3},{8,12},{9,13},{10,... | collective-permute-start | bytes 2064392 | tf_op jit(solution)/shard_map/ppermute | solution.py:275
  26.2 2.4 %cut.4 = (bf16[192,1792]{1,0:T(8,128)(2,1)}, bf16[192,1792]{1,0:T(8,128)(2,1)}) custom-call(bf16[64,7168]{1,0:T(8,128)(2,1)} %bitcast.13, bf16[64,7168]{1,0:T(8,128)(2,1)} %bitcast.16, bf16[64,7168]{1,0:T(8,128)(2,1)} %bitcast.19), custom_call_target="tpu_custom_call" | custom-call | tf_op jit(solution)/shard_map/cut/pallas_call | solution.py:132
  28.6 2.6 %collective-permute-start.1 = (bf16[192,1792]{1,0:T(8,128)(2,1)}, bf16[192,1792]{1,0:T(8,128)(2,1)S(1)}, u32[]{:S(2)}, u32[]{:S(2)}) collective-permute-start(bf16[192,1792]{1,0:T(8,128)(2,1)} %get-tuple-element.14), channel_id=1, source_target_pairs={{0,2},{1,3},{2,4},{3,5},{4,6},{5,7},{6,0},{7,1},{8,10},{9,11},{10,... | collective-permute-start | bytes 2064392 | tf_op jit(solution)/shard_map/ppermute | solution.py:275
  31.2 4.5 %collective-permute-start.3 = (bf16[192,1792]{1,0:T(8,128)(2,1)}, bf16[192,1792]{1,0:T(8,128)(2,1)S(1)}, u32[]{:S(2)}, u32[]{:S(2)}) collective-permute-start(bf16[192,1792]{1,0:T(8,128)(2,1)} %get-tuple-element.16), channel_id=1, source_target_pairs={{0,6},{1,7},{2,0},{3,1},{4,2},{5,3},{6,4},{7,5},{8,14},{9,15},{10,... | collective-permute-start | bytes 2064392 | tf_op jit(solution)/shard_map/ppermute | solution.py:275
  35.7 14.2 %all-to-all-done = bf16[64,4,896]{2,1,0:T(4,128)(2,1)S(1)} async-done(((bf16[64,4,896]{2,1,0:T(4,128)(2,1)}), bf16[64,4,896]{2,1,0:T(4,128)(2,1)S(1)}, u32[]{:S(2)}, u32[]{:S(2)}) %all-to-all-start) | async-done | bytes 458784 | tf_op jit(solution)/shard_map/all_to_all | solution.py:278
  49.9 0.2 copy.9
  50.0 0.9 reshape.10.rows_ref
  50.9 1.9 %collective-permute-start = (bf16[256,896]{1,0:T(8,128)(2,1)}, bf16[256,896]{1,0:T(8,128)(2,1)S(1)}, u32[]{:S(2)}, u32[]{:S(2)}) collective-permute-start(bf16[256,896]{1,0:T(8,128)(2,1)} %reshape.10.rows_ref), channel_id=1, source_target_pairs={{0,1},{1,0},{2,3},{3,2},{4,5},{5,4},{6,7},{7,6},{8,9},{9,8},{10,11... | collective-permute-start | bytes 1376264 | tf_op jit(solution)/shard_map/ppermute | solution.py:283
  52.8 1.9 %cut.3.refs_0_ = bf16[128,1792]{1,0:T(8,128)(2,1)} custom-call(bf16[64,7168]{1,0:T(8,128)(2,1)} %bitcast.14, bf16[64,7168]{1,0:T(8,128)(2,1)} %bitcast.17), custom_call_target="tpu_custom_call" | custom-call | tf_op jit(solution)/shard_map/cut/pallas_call | solution.py:132
  54.7 1.7 %cut.5.refs_0_ = bf16[64,1792]{1,0:T(8,128)(2,1)} custom-call(bf16[64,7168]{1,0:T(8,128)(2,1)} %bitcast.20), custom_call_target="tpu_custom_call" | custom-call | tf_op jit(solution)/shard_map/cut/pallas_call | solution.py:132
  56.4 0.0 copy-start
  56.4 0.0 collective-permute-done.2.refs_2_
  56.4 0.0 collective-permute-done.1.refs_1_
  56.4 0.0 collective-permute-done.3.refs_3_
  56.4 0.0 copy-start.1
  56.4 1.0 copy-done.1
  57.4 0.8 core_cut.1
  58.3 2.4 %collective-permute-start.4 = (bf16[256,896]{1,0:T(8,128)(2,1)}, bf16[256,896]{1,0:T(8,128)(2,1)S(1)}, u32[]{:S(2)}, u32[]{:S(2)}) collective-permute-start(bf16[256,896]{1,0:T(8,128)(2,1)} %get-tuple-element.20), channel_id=1, source_target_pairs={{0,1},{1,0},{2,3},{3,2},{4,5},{5,4},{6,7},{7,6},{8,9},{9,8},{10,11... | collective-permute-start | bytes 1376264 | tf_op jit(solution)/shard_map/ppermute | solution.py:214
  60.7 0.0 copy-done
  60.7 1.7 %near.1.near_ref = f32[4,128,256]{2,1,0:T(8,128)S(1)} custom-call(bf16[256,896]{1,0:T(8,128)(2,1)} %reshape.10.rows_ref, bf16[128,1792]{1,0:T(8,128)(2,1)S(1)} %copy-done, bf16[192,1792]{1,0:T(8,128)(2,1)S(1)} %collective-permute-done.1.refs_1_, bf16[192,1792]{1,0:T(8,128)(2,1)S(1)} %collective-permute-done.2.refs_2_, ...), custom_call_target="tpu_custom_call" | custom-call | flops 1000000000 | bytes 1000000 | tf_op jit(solution)/shard_map/near/pallas_call | solution.py:284
  62.4 0.0 collective-permute-done.rows_ref
  62.4 1.4 %far.1 = bf16[4,128,256]{2,1,0:T(8,128)(2,1)} custom-call(bf16[256,896]{1,0:T(8,128)(2,1)S(1)} %collective-permute-done.rows_ref, f32[4,128,256]{2,1,0:T(8,128)S(1)} %near.1.near_ref, bf16[128,1792]{1,0:T(8,128)(2,1)S(1)} %copy-done, bf16[192,1792]{1,0:T(8,128)(2,1)S(1)} %collective-permute-done.1.refs_1_, ...), custom_call_target="tpu_custom_call" | custom-call | tf_op jit(solution)/shard_map/far/pallas_call | solution.py:291
  63.8 0.0 copy-start.2
  63.9 0.0 copy-start.3
  63.9 4.5 %all-to-all-start.1 = ((bf16[4,128,256]{2,1,0:T(8,128)(2,1)}), bf16[4,128,256]{2,1,0:T(8,128)(2,1)S(1)}, u32[]{:S(2)}, u32[]{:S(2)}) async-start(bf16[4,128,256]{2,1,0:T(8,128)(2,1)} %far.1), calls=%async_computation.1 | async-start | bytes 524288 | tf_op jit(solution)/shard_map/all_to_all | solution.py:303
  68.4 0.0 copy-done.2
  68.4 0.0 copy-done.3
  68.4 0.2 mix.1.mix_ref
  68.6 6.6 %all-to-all-done.1.partial_ref = bf16[4,128,256]{2,1,0:T(8,128)(2,1)S(1)} async-done(((bf16[4,128,256]{2,1,0:T(8,128)(2,1)}), bf16[4,128,256]{2,1,0:T(8,128)(2,1)S(1)}, u32[]{:S(2)}, u32[]{:S(2)}) %all-to-all-start.1) | async-done | bytes 262176 | tf_op jit(solution)/shard_map/all_to_all | solution.py:303
  75.2 0.8 hidden.1
  76.0 3.4 %all-to-all-start.2 = ((bf16[8,64,256]{2,1,0:T(8,128)(2,1)}), bf16[8,64,256]{2,1,0:T(8,128)(2,1)S(1)}, u32[]{:S(2)}, u32[]{:S(2)}) async-start(bf16[8,64,256]{2,1,0:T(8,128)(2,1)} %hidden.1), calls=%async_computation.2 | async-start | bytes 524288 | tf_op jit(solution)/shard_map/all_to_all | solution.py:313
  79.4 0.0 collective-permute-done.4.refs_2_
  79.4 7.4 %all-to-all-done.2.refs_0_ = bf16[8,64,256]{2,1,0:T(8,128)(2,1)S(1)} async-done(((bf16[8,64,256]{2,1,0:T(8,128)(2,1)}), bf16[8,64,256]{2,1,0:T(8,128)(2,1)S(1)}, u32[]{:S(2)}, u32[]{:S(2)}) %all-to-all-start.2) | async-done | bytes 262176 | tf_op jit(solution)/shard_map/all_to_all | solution.py:313
  86.8 0.4 down.3
  87.2 3.0 %collective-permute-start.5 = (bf16[32,4,896]{2,1,0:T(4,128)(2,1)S(1)}, bf16[32,4,896]{2,1,0:T(4,128)(2,1)S(1)}, u32[]{:S(2)}, u32[]{:S(2)}) collective-permute-start(bf16[32,4,896]{2,1,0:T(4,128)(2,1)S(1)} %down.3), channel_id=1, source_target_pairs={{0,8},{8,0},{16,24},{24,16},{32,40},{40,32},{48,56},{56,48},{64,72... | collective-permute-start | bytes 688136 | tf_op jit(solution)/shard_map/ppermute | solution.py:328
  90.2 0.4 down.2
  90.6 5.5 %collective-permute-done.5 = bf16[32,4,896]{2,1,0:T(4,128)(2,1)S(1)} collective-permute-done((bf16[32,4,896]{2,1,0:T(4,128)(2,1)S(1)}, bf16[32,4,896]{2,1,0:T(4,128)(2,1)S(1)}, u32[]{:S(2)}, u32[]{:S(2)}) %collective-permute-start.5) | collective-permute-done | bytes 229408 | tf_op jit(solution)/shard_map/ppermute | solution.py:328
  96.1 0.1 add_convert_fusion
  96.2 30.8 %all_to_all.20 = bf16[32,4,896]{2,1,0:T(4,128)(2,1)S(1)} all-to-all(bf16[32,4,896]{2,1,0:T(4,128)(2,1)S(1)} %add_convert_fusion), channel_id=1, replica_groups={{0,16,32,48,64,80,96,112,128,144,160,176,192,208,224,240,256,272,288,30..., dimensions={0} | all-to-all | bytes 458752 | tf_op jit(solution)/shard_map/all_to_all | solution.py:332
  127.0 0.1 reshape.11.rows_ref
  127.0 0.8 combine.1
Async XLA Ops:
  2.3 47.6 %all-to-all-start = ((bf16[64,4,896]{2,1,0:T(4,128)(2,1)}), bf16[64,4,896]{2,1,0:T(4,128)(2,1)S(1)}, u32[]{:S(2)}, u32[]{:S(2)}) async-start(bf16[64,4,896]{2,1,0:T(4,128)(2,1)} %get-tuple-element.13), calls=%async_computation | async-start | bytes 917504 | tf_op jit(solution)/shard_map/all_to_all | solution.py:278
  21.1 35.3 %collective-permute-start.2 = (bf16[192,1792]{1,0:T(8,128)(2,1)}, bf16[192,1792]{1,0:T(8,128)(2,1)S(1)}, u32[]{:S(2)}, u32[]{:S(2)}) collective-permute-start(bf16[192,1792]{1,0:T(8,128)(2,1)} %get-tuple-element.15), channel_id=1, source_target_pairs={{0,4},{1,5},{2,6},{3,7},{4,0},{5,1},{6,2},{7,3},{8,12},{9,13},{10,... | collective-permute-start | bytes 2064392 | tf_op jit(solution)/shard_map/ppermute | solution.py:275
  28.6 27.8 %collective-permute-start.1 = (bf16[192,1792]{1,0:T(8,128)(2,1)}, bf16[192,1792]{1,0:T(8,128)(2,1)S(1)}, u32[]{:S(2)}, u32[]{:S(2)}) collective-permute-start(bf16[192,1792]{1,0:T(8,128)(2,1)} %get-tuple-element.14), channel_id=1, source_target_pairs={{0,2},{1,3},{2,4},{3,5},{4,6},{5,7},{6,0},{7,1},{8,10},{9,11},{10,... | collective-permute-start | bytes 2064392 | tf_op jit(solution)/shard_map/ppermute | solution.py:275
  31.2 25.3 %collective-permute-start.3 = (bf16[192,1792]{1,0:T(8,128)(2,1)}, bf16[192,1792]{1,0:T(8,128)(2,1)S(1)}, u32[]{:S(2)}, u32[]{:S(2)}) collective-permute-start(bf16[192,1792]{1,0:T(8,128)(2,1)} %get-tuple-element.16), channel_id=1, source_target_pairs={{0,6},{1,7},{2,0},{3,1},{4,2},{5,3},{6,4},{7,5},{8,14},{9,15},{10,... | collective-permute-start | bytes 2064392 | tf_op jit(solution)/shard_map/ppermute | solution.py:275
  50.9 11.5 %collective-permute-start = (bf16[256,896]{1,0:T(8,128)(2,1)}, bf16[256,896]{1,0:T(8,128)(2,1)S(1)}, u32[]{:S(2)}, u32[]{:S(2)}) collective-permute-start(bf16[256,896]{1,0:T(8,128)(2,1)} %reshape.10.rows_ref), channel_id=1, source_target_pairs={{0,1},{1,0},{2,3},{3,2},{4,5},{5,4},{6,7},{7,6},{8,9},{9,8},{10,11... | collective-permute-start | bytes 1376264 | tf_op jit(solution)/shard_map/ppermute | solution.py:283
  56.4 4.3 %copy-start = (bf16[128,1792]{1,0:T(8,128)(2,1)S(1)}, bf16[128,1792]{1,0:T(8,128)(2,1)}, u32[]{:S(2)}) copy-start(bf16[128,1792]{1,0:T(8,128)(2,1)} %cut.3.refs_0_) | copy-start | bytes 1376260
  56.4 1.0 copy-start.1
  58.3 21.1 %collective-permute-start.4 = (bf16[256,896]{1,0:T(8,128)(2,1)}, bf16[256,896]{1,0:T(8,128)(2,1)S(1)}, u32[]{:S(2)}, u32[]{:S(2)}) collective-permute-start(bf16[256,896]{1,0:T(8,128)(2,1)} %get-tuple-element.20), channel_id=1, source_target_pairs={{0,1},{1,0},{2,3},{3,2},{4,5},{5,4},{6,7},{7,6},{8,9},{9,8},{10,11... | collective-permute-start | bytes 1376264 | tf_op jit(solution)/shard_map/ppermute | solution.py:214
  63.8 4.5 %copy-start.2 = (s32[16,8]{0,1:T(8,128)S(1)}, s32[16,8]{0,1:T(8,128)}, u32[]{:S(2)}) copy-start(s32[16,8]{0,1:T(8,128)} %param.7) | copy-start | bytes 1540
  63.9 4.5 %copy-start.3 = (f32[16,8]{0,1:T(8,128)S(1)}, f32[16,8]{0,1:T(8,128)}, u32[]{:S(2)}) copy-start(f32[16,8]{0,1:T(8,128)} %param.8) | copy-start | bytes 1540
  63.9 11.3 %all-to-all-start.1 = ((bf16[4,128,256]{2,1,0:T(8,128)(2,1)}), bf16[4,128,256]{2,1,0:T(8,128)(2,1)S(1)}, u32[]{:S(2)}, u32[]{:S(2)}) async-start(bf16[4,128,256]{2,1,0:T(8,128)(2,1)} %far.1), calls=%async_computation.1 | async-start | bytes 524288 | tf_op jit(solution)/shard_map/all_to_all | solution.py:303
  76.0 10.8 %all-to-all-start.2 = ((bf16[8,64,256]{2,1,0:T(8,128)(2,1)}), bf16[8,64,256]{2,1,0:T(8,128)(2,1)S(1)}, u32[]{:S(2)}, u32[]{:S(2)}) async-start(bf16[8,64,256]{2,1,0:T(8,128)(2,1)} %hidden.1), calls=%async_computation.2 | async-start | bytes 524288 | tf_op jit(solution)/shard_map/all_to_all | solution.py:313
  87.2 8.9 %collective-permute-start.5 = (bf16[32,4,896]{2,1,0:T(4,128)(2,1)S(1)}, bf16[32,4,896]{2,1,0:T(4,128)(2,1)S(1)}, u32[]{:S(2)}, u32[]{:S(2)}) collective-permute-start(bf16[32,4,896]{2,1,0:T(4,128)(2,1)S(1)} %down.3), channel_id=1, source_target_pairs={{0,8},{8,0},{16,24},{24,16},{32,40},{40,32},{48,56},{56,48},{64,72... | collective-permute-start | bytes 688136 | tf_op jit(solution)/shard_map/ppermute | solution.py:328

commit v5 on v4

--- a/solution.py
+++ b/solution.py
@@ -163,20 +163,12 @@
 
 
 def far_kernel(rows_ref, near_ref, *refs):
-    *blocks, out_ref, held, given = refs
-    rings = len(blocks)
+    *blocks, out_ref = refs
     chip, core = lax.axis_index("tensor") // CORES, lax.rem(lax.axis_index("tensor"), CORES)
-    writes = []
     for ring, block in enumerate(blocks):
-        source = lax.rem(chip - ring + rings, rings)
-        total = near_ref[source] + half_product(
-            block, rows_ref, 1 - core, near_ref.shape[1]
-        )
-        held[ring] = total.astype(BF16)
-        writes.append(pltpu.make_async_copy(held.at[ring], out_ref.at[source], given.at[ring]))
-        writes[-1].start()
-    for write in writes:
-        write.wait()
+        source = lax.rem(chip - ring + len(blocks), len(blocks))
+        product = half_product(block, rows_ref, 1 - core, near_ref.shape[1])
+        out_ref[source] = (near_ref[source] + product).astype(BF16)
 
 
 def hidden_kernel(partial_ref, out_ref):
@@ -280,6 +272,7 @@
     arrived = jnp.swapaxes(arrived, 0, 1).reshape(arrived_count, width)
     down_near, down_far = down_columns([own_down, *blocks[1:]], width, groups)
 
+    arrived, mix = lax.optimization_barrier((arrived, mix))
     partner = lax.ppermute(arrived, "tensor", shift_pairs(groups, 0, 1))
     near = pl.pallas_call(
         near_kernel,
@@ -291,11 +284,6 @@
     partial = pl.pallas_call(
         far_kernel,
         out_shape=jax.ShapeDtypeStruct((rings, 2 * units, arrived_count), BF16),
-        out_specs=whole,
-        scratch_shapes=[
-            pltpu.VMEM((rings, 2 * units, arrived_count), BF16),
-            pltpu.SemaphoreType.DMA((rings,)),
-        ],
         compiler_params=pltpu.CompilerParams(vmem_limit_bytes=VMEM_BYTES),
         name="far",
     )(partner, near, *blocks)
@@ -309,7 +297,6 @@
         compiler_params=pltpu.CompilerParams(vmem_limit_bytes=VMEM_BYTES),
         name="hidden",
     )(partial)
-    hidden, mix = lax.optimization_barrier((hidden, mix))
     hidden = lax.all_to_all(hidden, "tensor", 0, 0, tiled=True)
 
     def product(other):

time: 130 us -> 129 us (level)
  blocking collectives: 30.8 us -> 41.9 us
  waiting for transfers between devices: 33.8 us -> 26.9 us
  starting transfers between devices: 46.2 us -> 41.7 us
    all_to_all x0 -> x1, blocking collectives: none -> 11.1 us  [body(): lax.all_to_all(partial, 'tensor', 0, 0, axis_index_groups=same_core, tile...]
    all_to_all x1 -> x0, waiting for transfers between devices: 6.65 us -> none  [body(): lax.all_to_all(partial, 'tensor', 0, 0, axis_index_groups=same_core, tile...]
    all_to_all x1 -> x0, starting transfers between devices: 4.49 us -> none  [body(): lax.all_to_all(partial, 'tensor', 0, 0, axis_index_groups=same_core, tile...]
  transfers between devices with their start and end apart: 9 -> 8, of which waited for: 4 -> 3; matrix products, arithmetic and copies ran while one was open for 1% -> 1% of each run, Pallas kernels for 9% -> 8%
where the time goes in v5:
time: 129 us; the launch traced here: 127 us
  blocking collectives  41.9 us (32%)
  starting transfers between devices  41.7 us (32%)
  waiting for transfers between devices  26.9 us (21%)
  Pallas kernels  14 us (11%)
  local copies, waits for them, and re-layouts  2.09 us (2%)
    all_to_all x1, blocking collectives, body(): lax.all_to_all(both, 'expert', 0, 0, axis_index_groups=same_half, tiled=T...  30.8 us
    all_to_all x1, starting transfers between devices, body(): arrived = lax.all_to_all(packed, 'expert', 0, 0, tiled=True)  18.8 us
    all_to_all x1, waiting for transfers between devices, body(): arrived = lax.all_to_all(packed, 'expert', 0, 0, tiled=True)  14 us
    ppermute x3, starting transfers between devices, body(): lax.ppermute(blocks[ring], 'tensor', shift_pairs(groups, ring, 0))  12.2 us
    all_to_all x1, blocking collectives, body(): lax.all_to_all(partial, 'tensor', 0, 0, axis_index_groups=same_core, tile...  11.1 us
    all_to_all x1, waiting for transfers between devices, body(): hidden = lax.all_to_all(hidden, 'tensor', 0, 0, tiled=True)  7.42 us
    pallas_call x3, Pallas kernels, cut(): pl.pallas_call(lambda *refs: cut_kernel(rings, *refs), out_shape=[shape]...  5.92 us
    ppermute x1, waiting for transfers between devices, body(): taken = lax.ppermute(product(1), 'expert', pairs)  5.49 us
  transfers between devices with their start and end apart: 8, of which 3 were waited for; matrix products, arithmetic and copies ran while one was open for 1% of the time, Pallas kernels for 8%

profile of v5, /device:TPU:6, one launch (start us, length us, event | category | flops | bytes accessed | tf_op | source)
XLA Modules:
  0.0 126.9 jit_solution(14425489432915889828)
XLA Ops:
  0.0 2.3 %pack.1 = (bf16[64,4,896]{2,1,0:T(4,128)(2,1)}, bf16[192,1792]{1,0:T(8,128)(2,1)}) custom-call(s32[8,16]{1,0:T(8,128)} %bitcast.9, bf16[16,896]{1,0:T(8,128)(2,1)} %refs_1_.1, bf16[64,7168]{1,0:T(8,128)(2,1)} %bitcast.12, bf16[64,7168]{1,0:T(8,128)(2,1)} %bitcast.15, bf16[64,7168]{1,0:T(8,128)(2,1)} %bitcast.18), custom_call_target="tpu_custom_call" | custom-call | tf_op jit(solution)/shard_map/pack/pallas_call | solution.py:239
  2.3 18.8 %all-to-all-start = ((bf16[64,4,896]{2,1,0:T(4,128)(2,1)}), bf16[64,4,896]{2,1,0:T(4,128)(2,1)S(1)}, u32[]{:S(2)}, u32[]{:S(2)}) async-start(bf16[64,4,896]{2,1,0:T(4,128)(2,1)} %get-tuple-element.13), calls=%async_computation | async-start | bytes 917504 | tf_op jit(solution)/shard_map/all_to_all | solution.py:270
  21.1 5.1 %collective-permute-start.2 = (bf16[192,1792]{1,0:T(8,128)(2,1)}, bf16[192,1792]{1,0:T(8,128)(2,1)S(1)}, u32[]{:S(2)}, u32[]{:S(2)}) collective-permute-start(bf16[192,1792]{1,0:T(8,128)(2,1)} %get-tuple-element.17), channel_id=1, source_target_pairs={{0,4},{1,5},{2,6},{3,7},{4,0},{5,1},{6,2},{7,3},{8,12},{9,13},{10,... | collective-permute-start | bytes 2064392 | tf_op jit(solution)/shard_map/ppermute | solution.py:267
  26.2 0.0 copy-start.3
  26.2 2.4 %cut.4 = (bf16[192,1792]{1,0:T(8,128)(2,1)}, bf16[192,1792]{1,0:T(8,128)(2,1)}) custom-call(bf16[64,7168]{1,0:T(8,128)(2,1)} %bitcast.13, bf16[64,7168]{1,0:T(8,128)(2,1)} %bitcast.16, bf16[64,7168]{1,0:T(8,128)(2,1)} %bitcast.19), custom_call_target="tpu_custom_call" | custom-call | tf_op jit(solution)/shard_map/cut/pallas_call | solution.py:132
  28.6 0.0 copy-start.2
  28.6 2.6 %collective-permute-start.1 = (bf16[192,1792]{1,0:T(8,128)(2,1)}, bf16[192,1792]{1,0:T(8,128)(2,1)S(1)}, u32[]{:S(2)}, u32[]{:S(2)}) collective-permute-start(bf16[192,1792]{1,0:T(8,128)(2,1)} %get-tuple-element.16), channel_id=1, source_target_pairs={{0,2},{1,3},{2,4},{3,5},{4,6},{5,7},{6,0},{7,1},{8,10},{9,11},{10,... | collective-permute-start | bytes 2064392 | tf_op jit(solution)/shard_map/ppermute | solution.py:267
  31.2 4.5 %collective-permute-start.3 = (bf16[192,1792]{1,0:T(8,128)(2,1)}, bf16[192,1792]{1,0:T(8,128)(2,1)S(1)}, u32[]{:S(2)}, u32[]{:S(2)}) collective-permute-start(bf16[192,1792]{1,0:T(8,128)(2,1)} %get-tuple-element.18), channel_id=1, source_target_pairs={{0,6},{1,7},{2,0},{3,1},{4,2},{5,3},{6,4},{7,5},{8,14},{9,15},{10,... | collective-permute-start | bytes 2064392 | tf_op jit(solution)/shard_map/ppermute | solution.py:267
  35.7 0.0 copy-done.3
  35.7 0.0 copy-done.2
  35.7 0.2 mix.1.mix_ref
  35.9 14.0 %all-to-all-done = bf16[64,4,896]{2,1,0:T(4,128)(2,1)S(1)} async-done(((bf16[64,4,896]{2,1,0:T(4,128)(2,1)}), bf16[64,4,896]{2,1,0:T(4,128)(2,1)S(1)}, u32[]{:S(2)}, u32[]{:S(2)}) %all-to-all-start) | async-done | bytes 458784 | tf_op jit(solution)/shard_map/all_to_all | solution.py:270
  49.9 0.2 copy.9
  50.0 0.9 reshape.10.rows_ref
  50.9 1.9 %collective-permute-start = (bf16[256,896]{1,0:T(8,128)(2,1)}, bf16[256,896]{1,0:T(8,128)(2,1)S(1)}, u32[]{:S(2)}, u32[]{:S(2)}) collective-permute-start(bf16[256,896]{1,0:T(8,128)(2,1)} %reshape.10.rows_ref), channel_id=1, source_target_pairs={{0,1},{1,0},{2,3},{3,2},{4,5},{5,4},{6,7},{7,6},{8,9},{9,8},{10,11... | collective-permute-start | bytes 1376264 | tf_op jit(solution)/shard_map/ppermute | solution.py:276
  52.8 1.9 %cut.3.refs_0_ = bf16[128,1792]{1,0:T(8,128)(2,1)} custom-call(bf16[64,7168]{1,0:T(8,128)(2,1)} %bitcast.14, bf16[64,7168]{1,0:T(8,128)(2,1)} %bitcast.17), custom_call_target="tpu_custom_call" | custom-call | tf_op jit(solution)/shard_map/cut/pallas_call | solution.py:132
  54.7 1.7 %cut.5.refs_0_ = bf16[64,1792]{1,0:T(8,128)(2,1)} custom-call(bf16[64,7168]{1,0:T(8,128)(2,1)} %bitcast.20), custom_call_target="tpu_custom_call" | custom-call | tf_op jit(solution)/shard_map/cut/pallas_call | solution.py:132
  56.4 0.0 copy-start
  56.4 0.0 collective-permute-done.2.refs_2_
  56.4 0.0 collective-permute-done.1.refs_1_
  56.4 0.0 collective-permute-done.3.refs_3_
  56.4 0.0 copy-start.1
  56.4 1.0 copy-done.1
  57.4 0.8 core_cut.1
  58.3 2.4 %collective-permute-start.4 = (bf16[256,896]{1,0:T(8,128)(2,1)}, bf16[256,896]{1,0:T(8,128)(2,1)S(1)}, u32[]{:S(2)}, u32[]{:S(2)}) collective-permute-start(bf16[256,896]{1,0:T(8,128)(2,1)} %get-tuple-element.20), channel_id=1, source_target_pairs={{0,1},{1,0},{2,3},{3,2},{4,5},{5,4},{6,7},{7,6},{8,9},{9,8},{10,11... | collective-permute-start | bytes 1376264 | tf_op jit(solution)/shard_map/ppermute | solution.py:206
  60.7 0.0 copy-done
  60.7 1.7 %near.1.near_ref = f32[4,128,256]{2,1,0:T(8,128)S(1)} custom-call(bf16[256,896]{1,0:T(8,128)(2,1)} %reshape.10.rows_ref, bf16[128,1792]{1,0:T(8,128)(2,1)S(1)} %copy-done, bf16[192,1792]{1,0:T(8,128)(2,1)S(1)} %collective-permute-done.1.refs_1_, bf16[192,1792]{1,0:T(8,128)(2,1)S(1)} %collective-permute-done.2.refs_2_, ...), custom_call_target="tpu_custom_call" | custom-call | flops 1000000000 | bytes 1000000 | tf_op jit(solution)/shard_map/near/pallas_call | solution.py:277
  62.4 0.0 collective-permute-done.rows_ref
  62.4 0.7 far.1
  63.2 11.1 %all_to_all.20.partial_ref = bf16[4,128,256]{2,1,0:T(8,128)(2,1)S(1)} all-to-all(bf16[4,128,256]{2,1,0:T(8,128)(2,1)S(1)} %far.1), channel_id=1, replica_groups={{0,2,4,6},{1,3,5,7},{8,10,12,14},{9,11,13,15},{16,18,20,22},{17,19,21,2..., dimensions={0} | all-to-all | bytes 524288 | tf_op jit(solution)/shard_map/all_to_all | solution.py:291
  74.3 0.7 hidden.1
  75.0 3.4 %all-to-all-start.2 = ((bf16[8,64,256]{2,1,0:T(8,128)(2,1)}), bf16[8,64,256]{2,1,0:T(8,128)(2,1)S(1)}, u32[]{:S(2)}, u32[]{:S(2)}) async-start(bf16[8,64,256]{2,1,0:T(8,128)(2,1)} %hidden.1), calls=%async_computation.2 | async-start | bytes 524288 | tf_op jit(solution)/shard_map/all_to_all | solution.py:300
  78.4 0.0 collective-permute-done.4.refs_2_
  78.4 7.4 %all-to-all-done.2.refs_0_ = bf16[8,64,256]{2,1,0:T(8,128)(2,1)S(1)} async-done(((bf16[8,64,256]{2,1,0:T(8,128)(2,1)}), bf16[8,64,256]{2,1,0:T(8,128)(2,1)S(1)}, u32[]{:S(2)}, u32[]{:S(2)}) %all-to-all-start.2) | async-done | bytes 262176 | tf_op jit(solution)/shard_map/all_to_all | solution.py:300
  85.9 0.4 down.3
  86.2 3.0 %collective-permute-start.5 = (bf16[32,4,896]{2,1,0:T(4,128)(2,1)S(1)}, bf16[32,4,896]{2,1,0:T(4,128)(2,1)S(1)}, u32[]{:S(2)}, u32[]{:S(2)}) collective-permute-start(bf16[32,4,896]{2,1,0:T(4,128)(2,1)S(1)} %down.3), channel_id=1, source_target_pairs={{0,8},{8,0},{16,24},{24,16},{32,40},{40,32},{48,56},{56,48},{64,72... | collective-permute-start | bytes 688136 | tf_op jit(solution)/shard_map/ppermute | solution.py:315
  89.2 0.4 down.2
  89.6 5.5 %collective-permute-done.5 = bf16[32,4,896]{2,1,0:T(4,128)(2,1)S(1)} collective-permute-done((bf16[32,4,896]{2,1,0:T(4,128)(2,1)S(1)}, bf16[32,4,896]{2,1,0:T(4,128)(2,1)S(1)}, u32[]{:S(2)}, u32[]{:S(2)}) %collective-permute-start.5) | collective-permute-done | bytes 229408 | tf_op jit(solution)/shard_map/ppermute | solution.py:315
  95.1 0.1 add_convert_fusion
  95.2 30.8 %all_to_all.21 = bf16[32,4,896]{2,1,0:T(4,128)(2,1)S(1)} all-to-all(bf16[32,4,896]{2,1,0:T(4,128)(2,1)S(1)} %add_convert_fusion), channel_id=1, replica_groups={{0,16,32,48,64,80,96,112,128,144,160,176,192,208,224,240,256,272,288,30..., dimensions={0} | all-to-all | bytes 458752 | tf_op jit(solution)/shard_map/all_to_all | solution.py:319
  126.0 0.1 reshape.11.rows_ref
  126.1 0.8 combine.1
Async XLA Ops:
  2.3 47.6 %all-to-all-start = ((bf16[64,4,896]{2,1,0:T(4,128)(2,1)}), bf16[64,4,896]{2,1,0:T(4,128)(2,1)S(1)}, u32[]{:S(2)}, u32[]{:S(2)}) async-start(bf16[64,4,896]{2,1,0:T(4,128)(2,1)} %get-tuple-element.13), calls=%async_computation | async-start | bytes 917504 | tf_op jit(solution)/shard_map/all_to_all | solution.py:270
  21.1 35.3 %collective-permute-start.2 = (bf16[192,1792]{1,0:T(8,128)(2,1)}, bf16[192,1792]{1,0:T(8,128)(2,1)S(1)}, u32[]{:S(2)}, u32[]{:S(2)}) collective-permute-start(bf16[192,1792]{1,0:T(8,128)(2,1)} %get-tuple-element.17), channel_id=1, source_target_pairs={{0,4},{1,5},{2,6},{3,7},{4,0},{5,1},{6,2},{7,3},{8,12},{9,13},{10,... | collective-permute-start | bytes 2064392 | tf_op jit(solution)/shard_map/ppermute | solution.py:267
  26.2 9.5 %copy-start.3 = (f32[16,8]{0,1:T(8,128)S(1)}, f32[16,8]{0,1:T(8,128)}, u32[]{:S(2)}) copy-start(f32[16,8]{0,1:T(8,128)} %param.8) | copy-start | bytes 1540
  28.6 7.1 %copy-start.2 = (s32[16,8]{0,1:T(8,128)S(1)}, s32[16,8]{0,1:T(8,128)}, u32[]{:S(2)}) copy-start(s32[16,8]{0,1:T(8,128)} %param.7) | copy-start | bytes 1540
  28.6 27.8 %collective-permute-start.1 = (bf16[192,1792]{1,0:T(8,128)(2,1)}, bf16[192,1792]{1,0:T(8,128)(2,1)S(1)}, u32[]{:S(2)}, u32[]{:S(2)}) collective-permute-start(bf16[192,1792]{1,0:T(8,128)(2,1)} %get-tuple-element.16), channel_id=1, source_target_pairs={{0,2},{1,3},{2,4},{3,5},{4,6},{5,7},{6,0},{7,1},{8,10},{9,11},{10,... | collective-permute-start | bytes 2064392 | tf_op jit(solution)/shard_map/ppermute | solution.py:267
  31.2 25.2 %collective-permute-start.3 = (bf16[192,1792]{1,0:T(8,128)(2,1)}, bf16[192,1792]{1,0:T(8,128)(2,1)S(1)}, u32[]{:S(2)}, u32[]{:S(2)}) collective-permute-start(bf16[192,1792]{1,0:T(8,128)(2,1)} %get-tuple-element.18), channel_id=1, source_target_pairs={{0,6},{1,7},{2,0},{3,1},{4,2},{5,3},{6,4},{7,5},{8,14},{9,15},{10,... | collective-permute-start | bytes 2064392 | tf_op jit(solution)/shard_map/ppermute | solution.py:267
  50.9 11.5 %collective-permute-start = (bf16[256,896]{1,0:T(8,128)(2,1)}, bf16[256,896]{1,0:T(8,128)(2,1)S(1)}, u32[]{:S(2)}, u32[]{:S(2)}) collective-permute-start(bf16[256,896]{1,0:T(8,128)(2,1)} %reshape.10.rows_ref), channel_id=1, source_target_pairs={{0,1},{1,0},{2,3},{3,2},{4,5},{5,4},{6,7},{7,6},{8,9},{9,8},{10,11... | collective-permute-start | bytes 1376264 | tf_op jit(solution)/shard_map/ppermute | solution.py:276
  56.4 4.3 %copy-start = (bf16[128,1792]{1,0:T(8,128)(2,1)S(1)}, bf16[128,1792]{1,0:T(8,128)(2,1)}, u32[]{:S(2)}) copy-start(bf16[128,1792]{1,0:T(8,128)(2,1)} %cut.3.refs_0_) | copy-start | bytes 1376260
  56.4 1.0 copy-start.1
  58.3 20.1 %collective-permute-start.4 = (bf16[256,896]{1,0:T(8,128)(2,1)}, bf16[256,896]{1,0:T(8,128)(2,1)S(1)}, u32[]{:S(2)}, u32[]{:S(2)}) collective-permute-start(bf16[256,896]{1,0:T(8,128)(2,1)} %get-tuple-element.20), channel_id=1, source_target_pairs={{0,1},{1,0},{2,3},{3,2},{4,5},{5,4},{6,7},{7,6},{8,9},{9,8},{10,11... | collective-permute-start | bytes 1376264 | tf_op jit(solution)/shard_map/ppermute | solution.py:206
  75.0 10.8 %all-to-all-start.2 = ((bf16[8,64,256]{2,1,0:T(8,128)(2,1)}), bf16[8,64,256]{2,1,0:T(8,128)(2,1)S(1)}, u32[]{:S(2)}, u32[]{:S(2)}) async-start(bf16[8,64,256]{2,1,0:T(8,128)(2,1)} %hidden.1), calls=%async_computation.2 | async-start | bytes 524288 | tf_op jit(solution)/shard_map/all_to_all | solution.py:300
  86.2 8.9 %collective-permute-start.5 = (bf16[32,4,896]{2,1,0:T(4,128)(2,1)S(1)}, bf16[32,4,896]{2,1,0:T(4,128)(2,1)S(1)}, u32[]{:S(2)}, u32[]{:S(2)}) collective-permute-start(bf16[32,4,896]{2,1,0:T(4,128)(2,1)S(1)} %down.3), channel_id=1, source_target_pairs={{0,8},{8,0},{16,24},{24,16},{32,40},{40,32},{48,56},{56,48},{64,72... | collective-permute-start | bytes 688136 | tf_op jit(solution)/shard_map/ppermute | solution.py:315
